TPU v7x, 32 devices: a whole 2x2x4 slice. The times are simulated.
32 devices in a mesh: seq: 8 (over z, y), tp: 4 (over x, core).
Axes of the slice: x: 2, y: 2, z: 4, core: 2. Of those that a mesh axis runs over, the one named last changes fastest.
Arguments:
- layer_activation: bfloat16 [3072, 2048], P('seq', 'tp'), may hold values from -6 to 6
- sequence_label: int32 [3072], P('seq'), may hold values from 0 to 2, as said below
- sequence_extents: int32 [2], replicated, may hold values from 1 to 1920, as said below
- destination_slots: int32 [2], replicated, may hold values from 0 to 7, as said below
- entry_layernorm_coef: float32 [2048], replicated, may hold values from 0.5 to 1.5
- lagged_blend_coefs: float32 [6, 2048], replicated, may hold values from 0 to 1
- query_matrix: bfloat16 [2048, 2048], P(None, 'tp'), may hold values from -0.125 to 0.125
- lookup_matrix: bfloat16 [2048, 2048], P(None, 'tp'), may hold values from -0.125 to 0.125
- content_matrix: bfloat16 [2048, 2048], P(None, 'tp'), may hold values from -0.125 to 0.125
- readout_matrix: bfloat16 [2048, 2048], P('tp'), may hold values from -0.125 to 0.125
- forgetting_narrow_matrix: bfloat16 [2048, 96], replicated, may hold values from -0.125 to 0.125
- forgetting_widen_matrix: bfloat16 [96, 2048], P(None, 'tp'), may hold values from -2.5 to 2.5
- forgetting_offset: float32 [2048], P('tp'), may hold values from -11 to -3.5
- stepsize_narrow_matrix: bfloat16 [2048, 96], replicated, may hold values from -0.125 to 0.125
- stepsize_widen_matrix: bfloat16 [96, 2048], P(None, 'tp'), may hold values from -0.625 to 0.625
- stepsize_offset: float32 [2048], P('tp'), may hold values from -4 to 4
- gating_narrow_matrix: bfloat16 [2048, 256], replicated, may hold values from -0.125 to 0.125
- gating_widen_matrix: bfloat16 [256, 2048], P(None, 'tp'), may hold values from -0.375 to 0.375
- erasure_lookup_coef: float32 [2048], P('tp'), may hold values from 0.5 to 1.5
- lookup_step_fraction: float32 [2048], P('tp'), may hold values from 0 to 1
- diagonal_reward_coef: float32 [2048], P('tp'), may hold values from -3 to 3
- group_layernorm_coef: float32 [2048], P('tp'), may hold values from 0.5 to 1.5
Outputs:
- mixed: bfloat16 [3072, 2048], P('seq', 'tp')
- final_states: float32 [8, 32, 64, 64], P('seq', 'tp')
- final_rows: bfloat16 [8, 2048], P('seq', 'tp')
Inputs may be any that keep to these rules, and one draw needn't show every extreme that they name: `sequence_label`: token p is in prompt 0 for p < sequence_extents[0], in prompt 1 for the next sequence_extents[1] tokens, and padding (2) after them; at least one padding token. `sequence_extents`: one length is exactly 1920, the other at least 768; their sum is under 3072. `destination_slots`: the two owners differ, and one of them is the last index of seq.
All inputs are finite; a program needn't handle non-finite values.
Results may differ from a plain program's by a relative error of at most 0.012.
Values may be sent and summed in bfloat16 or wider, within the bound.
A program may use at most 128 MiB of HBM per device.

v0:
```python
import jax
import jax.numpy as jnp
from jax import lax
from jax.sharding import PartitionSpec as P

CHANNELS_PER_ONE = 64
PROMPTS = 2


EPS = 1e-05
GROUP_EPS = 0.00064


def from_behind(array, axis, by):
    length = lax.axis_size(axis)
    pairs = [(i, i + by) for i in range(length) if 0 <= i + by < length]
    return lax.ppermute(array, axis, pairs)


def broadcast(value, axis, source):
    kept = jnp.where(lax.axis_index(axis) == source, value, 0).astype(value.dtype)
    return lax.psum(kept, axis)


def matmul(left, right):
    return jnp.dot(left, right, preferred_element_type=jnp.float32)


def compose(earlier_map, later_map):
    return jnp.einsum("hij,hjk->hik", earlier_map, later_map, precision=lax.Precision.HIGHEST)


def on_device(
    layer_activation,
    sequence_label,
    sequence_extents,
    destination_slots,
    entry_layernorm_coef,
    lagged_blend_coefs,
    query_matrix,
    lookup_matrix,
    content_matrix,
    readout_matrix,
    forgetting_narrow_matrix,
    forgetting_widen_matrix,
    forgetting_offset,
    stepsize_narrow_matrix,
    stepsize_widen_matrix,
    stepsize_offset,
    gating_narrow_matrix,
    gating_widen_matrix,
    erasure_lookup_coef,
    lookup_step_fraction,
    diagonal_reward_coef,
    group_layernorm_coef,
):
    highest = lax.Precision.HIGHEST
    segment_length = layer_activation.shape[0]
    stepsize_fraction = query_matrix.shape[1]
    local_attentioners = stepsize_fraction // CHANNELS_PER_ONE
    position = lax.axis_index("seq")
    column = lax.axis_index("tp")
    gathered = lax.all_gather(layer_activation, "tp", axis=1, tiled=True)
    floats = gathered.astype(jnp.float32)
    average = jnp.mean(floats, axis=1, keepdims=True)
    centred = floats - average
    variance = jnp.mean(centred * centred, axis=1, keepdims=True)
    normed = (centred * lax.rsqrt(variance + EPS) * entry_layernorm_coef).astype(jnp.bfloat16)
    normal_f = normed.astype(jnp.float32)
    arrived = from_behind(normed[-1:], "seq", 1)
    bounds = jnp.cumsum(sequence_extents)
    first_token = position * segment_length
    before = first_token - 1
    segment_before = (before >= bounds[0]).astype(jnp.int32) + (before >= bounds[1]).astype(
        jnp.int32
    )
    joined = (segment_before == sequence_label[0]) & (position > 0)
    continues = jnp.concatenate([joined[None], sequence_label[1:] == sequence_label[:-1]])
    previous = jnp.concatenate([arrived.astype(jnp.float32), normal_f[:-1]], axis=0)
    previous = jnp.where(continues[:, None], previous, jnp.zeros_like(previous))
    difference = previous - normal_f

    def blended(which):
        return (normal_f + difference * lagged_blend_coefs[which]).astype(jnp.bfloat16)

    receptance = matmul(blended(0), query_matrix)
    keys = matmul(blended(2), lookup_matrix)
    values = matmul(blended(3), content_matrix)
    decay_hidden = jnp.tanh(matmul(blended(1), forgetting_narrow_matrix)).astype(jnp.bfloat16)
    learn_hidden = matmul(blended(4), stepsize_narrow_matrix).astype(jnp.bfloat16)
    gate_hidden = jax.nn.sigmoid(matmul(blended(5), gating_narrow_matrix)).astype(jnp.bfloat16)
    log_rate = (
        -jax.nn.softplus(-(forgetting_offset + matmul(decay_hidden, forgetting_widen_matrix))) - 0.5
    )
    log_decay = -jnp.exp(log_rate)
    learning = jax.nn.sigmoid(stepsize_offset + matmul(learn_hidden, stepsize_widen_matrix))
    gating_signal = matmul(gate_hidden, gating_widen_matrix)
    removal = (keys * erasure_lookup_coef).reshape(
        segment_length, local_attentioners, CHANNELS_PER_ONE
    )
    removal = removal * lax.rsqrt(jnp.sum(removal * removal, axis=-1, keepdims=True) + 1e-06)
    written = keys * (1.0 + (learning - 1.0) * lookup_step_fraction)
    split_queries = receptance.reshape(segment_length, local_attentioners, CHANNELS_PER_ONE)
    split_lookups = written.reshape(segment_length, local_attentioners, CHANNELS_PER_ONE)
    split_contents = values.reshape(segment_length, local_attentioners, CHANNELS_PER_ONE)
    head_w = log_decay.reshape(segment_length, local_attentioners, CHANNELS_PER_ONE)
    head_a = learning.reshape(segment_length, local_attentioners, CHANNELS_PER_ONE)
    padded_v = jnp.concatenate([split_contents, jnp.zeros_like(split_contents)], axis=-1)
    local_ends = bounds - 1 - first_token
    block_len = min(64, segment_length)
    blocks = segment_length // block_len
    steps_in = jnp.arange(block_len, dtype=jnp.int32)
    strict_lower = steps_in[:, None] > steps_in[None, :]
    with_diag = steps_in[:, None] >= steps_in[None, :]
    unit_eye = jnp.eye(block_len, dtype=jnp.float32)

    def regroup(array):
        return array.reshape((blocks, block_len) + array.shape[1:])

    def block_step(carry, inputs):
        stacked, saved = carry
        block_start, still, r_blk, k_blk, v_blk, n_blk, lw_blk, a_blk = inputs
        restarts = jnp.logical_not(still).astype(jnp.int32)
        epochs = jnp.cumsum(restarts)
        from_start = (epochs == 0).astype(jnp.float32)
        log_total = jnp.cumsum(lw_blk, axis=0)
        query_a = -n_blk * jnp.exp(log_total - lw_blk)
        scaled_beta = n_blk * a_blk * jnp.exp(-log_total)
        scaled_key = k_blk * jnp.exp(-log_total)
        scaled_query = r_blk * jnp.exp(log_total)
        same_run = epochs[:, None] == epochs[None, :]
        strict_mask = (strict_lower & same_run).astype(jnp.float32)
        diag_mask = (with_diag & same_run).astype(jnp.float32)

        def paired(left, right, mask):
            return jnp.einsum("thj,shj->hts", left, right, precision=highest) * mask[None]

        mix_beta = paired(query_a, scaled_beta, strict_mask)
        mix_key = paired(query_a, scaled_key, strict_mask)
        read_beta = paired(scaled_query, scaled_beta, diag_mask)
        read_key = paired(scaled_query, scaled_key, diag_mask)
        from_state = jnp.einsum(
            "thj,hij->hti", query_a * from_start[:, None, None], stacked, precision=highest
        )
        right_side = from_state + jnp.einsum("hts,shi->hti", mix_key, v_blk, precision=highest)
        pseudo = jax.scipy.linalg.solve_triangular(
            unit_eye[None] - mix_beta, right_side, lower=True, unit_diagonal=True
        )
        outputs_blk = jnp.einsum(
            "thj,hij->thi", scaled_query * from_start[:, None, None], stacked, precision=highest
        )
        outputs_blk = outputs_blk + jnp.einsum("hts,hsi->thi", read_beta, pseudo, precision=highest)
        outputs_blk = outputs_blk + jnp.einsum("hts,shi->thi", read_key, v_blk, precision=highest)

        def state_at(moment):
            growth = jnp.exp(lax.dynamic_index_in_dim(log_total, moment, 0, keepdims=False))
            epoch_now = lax.dynamic_index_in_dim(epochs, moment, 0, keepdims=False)
            chosen = ((steps_in <= moment) & (epochs == epoch_now)).astype(jnp.float32)
            weight_beta = scaled_beta * chosen[:, None, None] * growth[None]
            weight_key = scaled_key * chosen[:, None, None] * growth[None]
            start_part = stacked * (growth * (epoch_now == 0).astype(jnp.float32))[:, None, :]
            result = start_part + jnp.einsum("hsi,shj->hij", pseudo, weight_beta, precision=highest)
            return result + jnp.einsum("shi,shj->hij", v_blk, weight_key, precision=highest)

        new_stacked = state_at(jnp.int32(block_len - 1))
        updated = []
        for prompt in range(PROMPTS):
            offset_end = local_ends[prompt] - block_start
            inside = (offset_end >= 0) & (offset_end < block_len)
            moment = jnp.clip(offset_end, 0, block_len - 1)
            updated.append(jnp.where(inside, state_at(moment), saved[prompt]))
        return ((new_stacked, jnp.stack(updated)), outputs_blk)

    identity = jnp.broadcast_to(
        jnp.eye(CHANNELS_PER_ONE, dtype=jnp.float32),
        (local_attentioners, CHANNELS_PER_ONE, CHANNELS_PER_ONE),
    )
    start_stack = jnp.concatenate([jnp.zeros_like(identity), identity], axis=1)
    start_saved = jnp.zeros(
        (PROMPTS, local_attentioners, 2 * CHANNELS_PER_ONE, CHANNELS_PER_ONE), jnp.float32
    )
    block_starts = jnp.arange(blocks, dtype=jnp.int32) * block_len
    scan_inputs = (
        block_starts,
        regroup(continues),
        regroup(split_queries),
        regroup(split_lookups),
        regroup(padded_v),
        regroup(removal),
        regroup(head_w),
        regroup(head_a),
    )
    (final_stack, saved), grouped_out = lax.scan(
        block_step, (start_stack, start_saved), scan_inputs
    )
    outputs = grouped_out.reshape(segment_length, local_attentioners, 2 * CHANNELS_PER_ONE)
    local_state = final_stack[:, :CHANNELS_PER_ONE]
    transition = final_stack[:, CHANNELS_PER_ONE:]

    def passing(turn, incoming):
        return from_behind(
            (compose(incoming, transition) + local_state).astype(jnp.bfloat16), "seq", 1
        ).astype(jnp.float32)

    state_in = lax.fori_loop(0, lax.axis_size("seq") - 1, passing, jnp.zeros_like(local_state))
    readout = outputs[:, :, :CHANNELS_PER_ONE] + jnp.einsum(
        "hij,thj->thi", state_in, outputs[:, :, CHANNELS_PER_ONE:], precision=highest
    )
    centre = readout - jnp.mean(readout, axis=-1, keepdims=True)
    spread = jnp.mean(centre * centre, axis=-1, keepdims=True)
    group_standardized = (
        centre
        * lax.rsqrt(spread + GROUP_EPS)
        * group_layernorm_coef.reshape(local_attentioners, CHANNELS_PER_ONE)
    )
    diagonal_reward = (
        jnp.sum(
            split_queries
            * split_lookups
            * diagonal_reward_coef.reshape(local_attentioners, CHANNELS_PER_ONE),
            axis=-1,
            keepdims=True,
        )
        * split_contents
    )
    visible_entries = (
        (group_standardized + diagonal_reward).reshape(segment_length, stepsize_fraction)
        * gating_signal
    ).astype(jnp.bfloat16)
    partial_value = matmul(visible_entries, readout_matrix)
    summed = lax.psum_scatter(
        partial_value.astype(jnp.bfloat16), "tp", scatter_dimension=1, tiled=True
    ).astype(jnp.float32)
    mixed = (summed + layer_activation.astype(jnp.float32)).astype(jnp.bfloat16)
    final_states = jnp.zeros(
        (1, local_attentioners, CHANNELS_PER_ONE, CHANNELS_PER_ONE), jnp.float32
    )
    final_rows = jnp.zeros((1, stepsize_fraction), jnp.bfloat16)
    for prompt in range(PROMPTS):
        last_token = bounds[prompt] - 1
        holder = last_token // segment_length
        inside = jnp.clip(last_token - first_token, 0, segment_length - 1)
        recorded = saved[prompt]
        state_end = (
            compose(state_in, recorded[:, CHANNELS_PER_ONE:]) + recorded[:, :CHANNELS_PER_ONE]
        )
        row_end = lax.dynamic_slice(
            normal_f, (inside, column * stepsize_fraction), (1, stepsize_fraction)
        )
        got_state, got_row = (
            broadcast(state_end.astype(jnp.bfloat16), "seq", holder).astype(state_end.dtype),
            broadcast(row_end.astype(jnp.bfloat16), "seq", holder).astype(row_end.dtype),
        )
        is_owner = position == destination_slots[prompt]
        final_states = jnp.where(is_owner, got_state[None], final_states)
        final_rows = jnp.where(is_owner, got_row.astype(jnp.bfloat16), final_rows)
    return (mixed, final_states, final_rows)


def solution(mesh):
    return jax.shard_map(
        on_device,
        mesh=mesh,
        in_specs=(
            P("seq", "tp"),
            P("seq"),
            P(),
            P(),
            P(),
            P(),
            P(None, "tp"),
            P(None, "tp"),
            P(None, "tp"),
            P("tp", None),
            P(),
            P(None, "tp"),
            P("tp"),
            P(),
            P(None, "tp"),
            P("tp"),
            P(),
            P(None, "tp"),
            P("tp"),
            P("tp"),
            P("tp"),
            P("tp"),
        ),
        out_specs=(P("seq", "tp"), P("seq", "tp", None, None), P("seq", "tp")),
        check_vma=False,
    )
```

profile of v0, /device:TPU:0, one launch (start us, length us, event | category | flops | bytes accessed | tf_op | source)
XLA Modules:
  0.0 698.0 jit_solution(5239069506846674704)
XLA Ops:
  14.6 17.4 %all-gather.2.cloned.1.call-done = bf16[384,2048]{1,0:T(8,128)(2,1)} async-done(((bf16[384,512]{1,0:T(8,128)(2,1)}), bf16[384,2048]{1,0:T(8,128)(2,1)}) %all-gather.2.cloned.1.call-update) | async-done | bytes 1572880 | tf_op jit(solution)/shard_map/all_gather | solution.py:63
  32.0 1.8 convert_reduce_fusion
  33.8 2.0 fusion.61
  37.5 3.4 collective-permute-start.1
  42.8 3.5 slice.133
  46.3 3.9 fusion.101
  51.7 5.1 fusion.72
  56.7 2.5 reshape_reshape.15
  59.3 5.5 fusion.149
  66.4 2.3 copy.125
  68.7 5.1 fusion.139
  73.8 2.7 reshape_reshape.12
  76.5 2.6 reshape.279
  80.6 4.5 fusion.74
  86.8 2.8 concatenate.15.clone
  89.6 1.7 broadcast_multiply_fusion.2
  92.1 414.9 %while.27 = (s32[]{:T(128)}, f32[8,128,64]{1,2,0:T(8,128)S(1)}, f32[2,8,128,64]{2,3,1,0:T(8,128)}, f32[6,64,8,128]{3,2,1,0:T(8,128)}, f32[6,64,8,64]{3,2,1,0:T(8...) while((s32[]{:T(128)}, f32[8,128,64]{1,2,0:T(8,128)S(1)}, ...), condition=%wide.region_7.8_spmd.clone.clone, body=%wide.region_4.7_spmd.clone.clone.sunk | while | flops 708762112 | bytes 20262212 | solution.py:193
  99.0 2.0 and_convert_fusion.4
  103.1 2.4 multiply_multiply_fusion.8
  108.9 40.7 %custom-call.9 = f32[8,1,64,64]{2,3,1,0:T(8,128)} custom-call(f32[8,1,64,64]{3,2,1,0:T(8,128)} %fusion.259), custom_call_target="InvertDiagBlocksLowerTriangular" | custom-call | tf_op jit(solution)/shard_map/while/body/eval_jaxpr/jit(_solve_triangular)/vmap()/triangular_solve | solution.py:146
  149.6 1.7 fusion.260
  168.1 2.0 and_convert_fusion.4
  172.3 2.4 multiply_multiply_fusion.8
  178.1 40.7 %custom-call.9 = f32[8,1,64,64]{2,3,1,0:T(8,128)} custom-call(f32[8,1,64,64]{3,2,1,0:T(8,128)} %fusion.259), custom_call_target="InvertDiagBlocksLowerTriangular" | custom-call | tf_op jit(solution)/shard_map/while/body/eval_jaxpr/jit(_solve_triangular)/vmap()/triangular_solve | solution.py:146
  237.3 2.0 and_convert_fusion.4
  241.4 2.4 multiply_multiply_fusion.8
  247.2 40.7 %custom-call.9 = f32[8,1,64,64]{2,3,1,0:T(8,128)} custom-call(f32[8,1,64,64]{3,2,1,0:T(8,128)} %fusion.259), custom_call_target="InvertDiagBlocksLowerTriangular" | custom-call | tf_op jit(solution)/shard_map/while/body/eval_jaxpr/jit(_solve_triangular)/vmap()/triangular_solve | solution.py:146
  306.4 2.0 and_convert_fusion.4
  310.6 2.4 multiply_multiply_fusion.8
  316.4 40.7 %custom-call.9 = f32[8,1,64,64]{2,3,1,0:T(8,128)} custom-call(f32[8,1,64,64]{3,2,1,0:T(8,128)} %fusion.259), custom_call_target="InvertDiagBlocksLowerTriangular" | custom-call | tf_op jit(solution)/shard_map/while/body/eval_jaxpr/jit(_solve_triangular)/vmap()/triangular_solve | solution.py:146
  375.6 2.0 and_convert_fusion.4
  379.8 2.4 multiply_multiply_fusion.8
  385.5 40.7 %custom-call.9 = f32[8,1,64,64]{2,3,1,0:T(8,128)} custom-call(f32[8,1,64,64]{3,2,1,0:T(8,128)} %fusion.259), custom_call_target="InvertDiagBlocksLowerTriangular" | custom-call | tf_op jit(solution)/shard_map/while/body/eval_jaxpr/jit(_solve_triangular)/vmap()/triangular_solve | solution.py:146
  444.8 2.0 and_convert_fusion.4
  448.9 2.4 multiply_multiply_fusion.8
  454.7 40.7 %custom-call.9 = f32[8,1,64,64]{2,3,1,0:T(8,128)} custom-call(f32[8,1,64,64]{3,2,1,0:T(8,128)} %fusion.259), custom_call_target="InvertDiagBlocksLowerTriangular" | custom-call | tf_op jit(solution)/shard_map/while/body/eval_jaxpr/jit(_solve_triangular)/vmap()/triangular_solve | solution.py:146
  495.4 1.7 fusion.260
  507.3 2.4 copy.127
  509.7 2.4 slice_bitcast_fusion.1
  512.1 2.1 fusion.152
  514.2 2.8 copy.135
  517.1 55.1 %while.28 = (s32[]{:T(128)}, f32[8,64,64]{2,1,0:T(8,128)S(1)}, f32[8,64,64]{2,1,0:T(8,128)S(1)}, f32[8,64,64]{2,1,0:T(8,128)S(1)}, s32[]{:T(128)}, /*index=5*/s32[]{:T(128)}) while((s32[]{:T(128)}, f32[8,64,64]{2,1,0:T(8,128)S(1)}, f32[8,64,64]{2,1,0:T(8,128)S(1)}, f32[8,64,64]{2,1,0:T(8,128)S(1)}, s32[]{:T(128)}, ...), condition=%wide.region_9.10_spmd.clone, body=%wide.region_8.9_spmd.clone.sunk | while | flops 25296900 | bytes 917623 | solution.py:205
  517.4 3.4 collective-permute-start
  520.8 2.8 collective-permute-done
  524.1 4.4 collective-permute-start
  528.5 2.5 collective-permute-done
  531.4 4.4 collective-permute-start
  535.8 2.5 collective-permute-done
  538.7 5.2 collective-permute-start
  543.9 2.5 collective-permute-done
  546.9 5.3 collective-permute-start
  552.1 2.5 collective-permute-done
  555.1 5.3 collective-permute-start
  560.3 3.0 collective-permute-done
  563.8 5.6 collective-permute-start
  569.4 2.5 collective-permute-done
  572.1 4.1 fusion.157
  579.0 4.4 fusion.116
  585.6 4.1 convolution_convert_fusion
  592.5 22.7 %all-reduce.2 = (bf16[1,512]{1,0:T(2,128)(2,1)S(1)}, bf16[1,512]{1,0:T(2,128)(2,1)S(1)}) all-reduce(bf16[1,512]{1,0:T(2,128)(2,1)S(1)} %get-tuple-element.333, bf16[1,512]{1,0:T(2,128)(2,1)S(1)} %get-tuple-element.332), channel_id=1, replica_groups=mesh['seq'=8,'tp'=4] {'seq'}, use_global_device_ids=true, to_apply=%region_16.17 | all-reduce | flops 1024 | bytes 4096 | tf_op jit(solution)/shard_map/psum | solution.py:22
  615.9 43.6 %all-reduce.6.cloned.1.call-done = (bf16[8,64,64]{2,1,0:T(8,128)(2,1)}, bf16[8,64,64]{2,1,0:T(8,128)(2,1)}) async-done(((bf16[8,64,64]{2,1,0:T(8,128)(2,1)}, bf16[8,64,64]{2,1,0:T(8,128)(2,1)}), (bf16[8,64,64]{2,1,0:T(8,128)(2,1)}, bf16[8,64,64]{2,1,0:T(8,128)(2,1)})) %all-reduce.6.cloned.1.call-update) | async-done | bytes 131088 | tf_op jit(solution)/shard_map/psum | solution.py:22
  659.4 1.7 select_bitcast_fusion
  661.1 28.5 %reduce-scatter.2.cloned.1.call-done = bf16[384,512]{1,0:T(8,128)(2,1)} async-done(((bf16[384,2048]{1,0:T(8,128)(2,1)}), bf16[384,512]{1,0:T(8,128)(2,1)}) %reduce-scatter.2.cloned.1.call-update) | async-done | bytes 393232 | tf_op jit(solution)/shard_map/reduce_scatter | solution.py:231
  689.6 1.8 add_convert_fusion
  (320 shorter events, 137.1 us)
Async XLA Ops:
  7.2 52.1 %copy-start = (bf16[2048,512]{1,0:T(8,128)(2,1)S(1)}, bf16[2048,512]{1,0:T(8,128)(2,1)}, u32[]{:S(2)}) copy-start(bf16[2048,512]{1,0:T(8,128)(2,1)} %param.33) | copy-start | bytes 6291460
  7.2 28.6 %copy-start.15 = (f32[2048]{0:T(1024)S(1)}, f32[2048]{0:T(1024)}, u32[]{:S(2)}) copy-start(f32[2048]{0:T(1024)} %param.30) | copy-start | bytes 24580
  7.2 24.8 %all-gather.2.cloned.1.call-start = ((), (), s32[]{:S(2)}) async-start(), calls=%async_computation.1 | async-start | bytes 1966080 | tf_op jit(solution)/shard_map/all_gather | solution.py:63
  7.9 651.5 %all-reduce.6.cloned.1.call-start = ((), (), s32[]{:S(2)}) async-start(), calls=%async_computation.3 | async-start | bytes 524288 | tf_op jit(solution)/shard_map/psum | solution.py:22
  14.6 27.9 %copy-start.16 = (f32[512]{0:T(512)S(1)}, f32[512]{0:T(512)}, u32[]{:S(2)}) copy-start(f32[512]{0:T(512)} %param.46) | copy-start | bytes 6148
  14.6 28.0 %copy-start.17 = (f32[512]{0:T(512)S(1)}, f32[512]{0:T(512)}, u32[]{:S(2)}) copy-start(f32[512]{0:T(512)} %param.47) | copy-start | bytes 6148
  32.0 3.8 copy-start.5
  36.3 1.2 copy-start.4
  37.5 8.7 %collective-permute-start.1 = (bf16[1,2048]{1,0:T(2,128)(2,1)S(1)}, bf16[1,2048]{1,0:T(2,128)(2,1)S(1)}, u32[]{:S(2)}, u32[]{:S(2)}) collective-permute-start(bf16[1,2048]{1,0:T(2,128)(2,1)S(1)} %slice.132), channel_id=1, source_target_pairs={{0,4},{4,8},{8,12},{12,16},{16,20},{20,24},{24,28},{1,5},{5,9},{9,... | collective-permute-start | bytes 12296 | tf_op jit(solution)/shard_map/ppermute | solution.py:17
  42.8 3.5 copy-start.19
  42.8 3.5 copy-start.20
  51.7 7.6 %copy-start.21 = (f32[512]{0:T(512)S(1)}, f32[512]{0:T(512)}, u32[]{:S(2)}) copy-start(f32[512]{0:T(512)} %param.44) | copy-start | bytes 6148
  51.7 7.6 %copy-start.22 = (f32[512]{0:T(512)S(1)}, f32[512]{0:T(512)}, u32[]{:S(2)}) copy-start(f32[512]{0:T(512)} %param.45) | copy-start | bytes 6148
  64.8 3.9 copy-start.23
  73.8 5.3 copy-start.14
  85.1 6.1 copy-start.9
  86.8 2.8 copy-start.7
  149.6 4.9 copy-start.1
  155.5 2.8 copy-start.2
  218.7 4.9 copy-start.1
  224.6 2.8 copy-start.2
  287.9 4.9 copy-start.1
  293.8 2.8 copy-start.2
  357.1 4.9 copy-start.1
  363.0 2.8 copy-start.2
  426.2 4.9 copy-start.1
  432.1 2.8 copy-start.2
  495.4 4.9 copy-start.1
  501.3 2.8 copy-start.2
  509.7 2.4 copy-start.6
  512.1 4.9 copy-start.3
  517.4 6.2 collective-permute-start
  524.1 6.9 collective-permute-start
  531.4 6.9 collective-permute-start
  538.7 7.7 %collective-permute-start = (bf16[8,64,64]{2,1,0:T(8,128)(2,1)S(1)}, bf16[8,64,64]{2,1,0:T(8,128)(2,1)S(1)}, u32[]{:S(2)}, u32[]{:S(2)}) collective-permute-start(bf16[8,64,64]{2,1,0:T(8,128)(2,1)S(1)} %fusion.267), channel_id=1, source_target_pairs={{0,4},{4,8},{8,12},{12,16},{16,20},{20,24},{24,28},{1,5},{5,9},{9,... | collective-permute-start | bytes 196616 | tf_op jit(solution)/shard_map/while/body/eval_jaxpr/ppermute | solution.py:17
  546.9 7.8 %collective-permute-start = (bf16[8,64,64]{2,1,0:T(8,128)(2,1)S(1)}, bf16[8,64,64]{2,1,0:T(8,128)(2,1)S(1)}, u32[]{:S(2)}, u32[]{:S(2)}) collective-permute-start(bf16[8,64,64]{2,1,0:T(8,128)(2,1)S(1)} %fusion.267), channel_id=1, source_target_pairs={{0,4},{4,8},{8,12},{12,16},{16,20},{20,24},{24,28},{1,5},{5,9},{9,... | collective-permute-start | bytes 196616 | tf_op jit(solution)/shard_map/while/body/eval_jaxpr/ppermute | solution.py:17
  555.1 8.3 %collective-permute-start = (bf16[8,64,64]{2,1,0:T(8,128)(2,1)S(1)}, bf16[8,64,64]{2,1,0:T(8,128)(2,1)S(1)}, u32[]{:S(2)}, u32[]{:S(2)}) collective-permute-start(bf16[8,64,64]{2,1,0:T(8,128)(2,1)S(1)} %fusion.267), channel_id=1, source_target_pairs={{0,4},{4,8},{8,12},{12,16},{16,20},{20,24},{24,28},{1,5},{5,9},{9,... | collective-permute-start | bytes 196616 | tf_op jit(solution)/shard_map/while/body/eval_jaxpr/ppermute | solution.py:17
  563.8 8.1 %collective-permute-start = (bf16[8,64,64]{2,1,0:T(8,128)(2,1)S(1)}, bf16[8,64,64]{2,1,0:T(8,128)(2,1)S(1)}, u32[]{:S(2)}, u32[]{:S(2)}) collective-permute-start(bf16[8,64,64]{2,1,0:T(8,128)(2,1)S(1)} %fusion.267), channel_id=1, source_target_pairs={{0,4},{4,8},{8,12},{12,16},{16,20},{20,24},{24,28},{1,5},{5,9},{9,... | collective-permute-start | bytes 196616 | tf_op jit(solution)/shard_map/while/body/eval_jaxpr/ppermute | solution.py:17
  572.1 4.3 copy-start.8
  572.1 4.3 copy-start.10
  579.0 4.4 copy-start.13
  579.0 5.5 copy-start.12
  585.6 4.2 copy-start.18
  585.6 104.1 %copy-start.11 = (bf16[384,512]{1,0:T(8,128)(2,1)S(1)}, bf16[384,512]{1,0:T(8,128)(2,1)}, u32[]{:S(2)}) copy-start(bf16[384,512]{1,0:T(8,128)(2,1)} %param.26) | copy-start | bytes 1179652
  585.6 104.0 %reduce-scatter.2.cloned.1.call-start = ((), (), s32[]{:S(2)}) async-start(), calls=%async_computation.2 | async-start | bytes 1966080 | tf_op jit(solution)/shard_map/reduce_scatter | solution.py:231
Sparse Core Ops, SparseCore 0:
  9.6 22.3 all-gather.1
  585.7 73.6 all-reduce.5
  662.1 27.4 reduce-scatter.1
where the time goes:
time: 701 us; the launch traced here: 698 us
  other arithmetic  299 us (43%)
  matrix products  120 us (17%)
  waiting for transfers between devices  109 us (16%)
  local copies, waits for them, and re-layouts  62.6 us (9%)
  starting transfers between devices  36.9 us (5%)
  loops' own time  29.5 us (4%)
  blocking collectives  22.7 us (3%)
  between operations  18.8 us (3%)
    another operation x18, other arithmetic, block_step(): jax.scipy.linalg.solve_triangular(unit_eye[None] - mix_beta, right_side,...  245 us
    psum x1, waiting for transfers between devices, broadcast(): return lax.psum(kept, axis)  43.6 us
    ppermute x8, starting transfers between devices, from_behind(): return lax.ppermute(array, axis, pairs)  36.8 us
    dot_general x7, matrix products, matmul(): return jnp.dot(left, right, preferred_element_type=jnp.float32)  32.6 us
    another operation x1, loops' own time, on_device(): lax.scan(block_step, (start_stack, start_saved), scan_inputs)  29.1 us
    reduce_scatter x1, waiting for transfers between devices, on_device(): lax.psum_scatter(partial_value.astype(jnp.bfloat16), 'tp', scatter_dimens...  28.5 us
    psum x1, blocking collectives, broadcast(): return lax.psum(kept, axis)  22.7 us
    dot_general x24, matrix products, paired(): jnp.einsum('thj,shj->hts', left, right, precision=highest) * mask[None]  18.6 us
  transfers between devices with their start and end apart: 11, of which 10 were waited for; matrix products, arithmetic and copies ran while one was open for 2% of the time, Pallas kernels for 0%

commit v1 on v0

v1 whole, which is shorter than its diff:
```python
import functools

import jax
import jax.numpy as jnp
from jax import lax
from jax.experimental import pallas as pl
from jax.experimental.pallas import tpu as pltpu
from jax.sharding import PartitionSpec as P

HEAD = 64
PAIR = 128
PROMPTS = 2
CHUNK = 64
EPS = 1e-05
GROUP_EPS = 0.00064
F32 = jnp.float32
BF16 = jnp.bfloat16
NN = (((1,), (0,)), ((), ()))
NT = (((1,), (1,)), ((), ()))
TN = (((0,), (0,)), ((), ()))


def split(x):
    high = x.astype(BF16)
    return high, (x - high.astype(F32)).astype(BF16)


def dot1(a, b, dims=NN):
    return lax.dot_general(a.astype(BF16), b.astype(BF16), dims, preferred_element_type=F32)


def dot3(a, b, dims=NN):
    ah, al = split(a)
    bh, bl = split(b)
    first = lax.dot_general(ah, bh, dims, preferred_element_type=F32)
    second = lax.dot_general(al, bh, dims, preferred_element_type=F32)
    third = lax.dot_general(ah, bl, dims, preferred_element_type=F32)
    return first + (second + third)


def dot_exact_right(a, b):
    ah, al = split(a)
    return lax.dot_general(
        jnp.concatenate([ah, al], axis=1),
        jnp.concatenate([b, b], axis=0),
        NN,
        preferred_element_type=F32,
    )


def head_ones():
    row = lax.broadcasted_iota(jnp.int32, (PAIR, PAIR), 0) // HEAD
    col = lax.broadcasted_iota(jnp.int32, (PAIR, PAIR), 1) // HEAD
    return (row == col).astype(BF16)


def two(x):
    lane = lax.broadcasted_iota(jnp.int32, x.shape, 1)
    zero = jnp.zeros_like(x)
    return jnp.concatenate(
        [jnp.where(lane < HEAD, x, zero), jnp.where(lane >= HEAD, x, zero)], axis=0
    )


def fold(x):
    return x[:HEAD] + x[HEAD:]


def chunk_kernel(
    scal_ref, r_ref, k_ref, v_ref, fl_ref, ll_ref, er_ref, fr_ref, rw_ref, epc_ref, epr_ref,
    y_ref, z_ref, bonus_ref, a_ref, b_ref, maps_ref, run_ref,
):
    c = pl.program_id(0)
    pairs = r_ref.shape[1] // PAIR
    e_in, e_last = scal_ref[c, 0], scal_ref[c, 1]
    inside, moment, e_end = scal_ref[c, 2], scal_ref[c, 3], scal_ref[c, 4]

    row = lax.broadcasted_iota(jnp.int32, (PAIR, PAIR), 0)
    col = lax.broadcasted_iota(jnp.int32, (PAIR, PAIR), 1)
    eye = (row == col).astype(F32)

    @pl.when(c == 0)
    def _():
        maps_ref[...] = jnp.zeros_like(maps_ref)
        for p in range(pairs):
            run_ref[p] = jnp.concatenate([eye, jnp.zeros_like(eye)], axis=0)

    epc = epc_ref[...]
    epc2 = jnp.concatenate([epc, epc], axis=0)
    epr = epr_ref[0, 0:1, :]
    same = (row // HEAD == col // HEAD) & (epc2 == epr)
    strict = same & (row > col)
    diag = same & (row >= col)
    ones = head_ones()
    tri = (
        lax.broadcasted_iota(jnp.int32, (CHUNK, CHUNK), 0)
        >= lax.broadcasted_iota(jnp.int32, (CHUNK, CHUNK), 1)
    ).astype(F32)

    lw_all = -0.6065306597126334 * jax.nn.sigmoid(fl_ref[...])
    lt_all = jnp.dot(tri, lw_all, precision=lax.Precision.HIGHEST, preferred_element_type=F32)
    learn_all = jax.nn.sigmoid(ll_ref[...])
    from_start = (epc2 == e_in).astype(F32)
    chosen = (epc2 == e_last).astype(F32)
    keep = jnp.where(e_last == e_in, 1.0, 0.0).astype(F32)
    sides = [slice(p * PAIR, (p + 1) * PAIR) for p in range(pairs)]
    keys, removals, writtens = [], [], []
    for s in sides:
        k = k_ref[:, s]
        kk = k * er_ref[0:1, s]
        ss = dot_exact_right(kk * kk, ones)
        removals.append(kk * lax.rsqrt(ss + 1e-06))
        writtens.append(k * (1.0 + (learn_all[:, s] - 1.0) * fr_ref[0:1, s]))
    grams, qas, qs, betas, keys, vvs, growths = [], [], [], [], [], [], []
    for p, s in enumerate(sides):
        lw, lt = lw_all[:, s], lt_all[:, s]
        n, w, r, v = removals[p], writtens[p], r_ref[:, s], v_ref[:, s]
        inv = jnp.exp(-lt)
        qa = -n * jnp.exp(lt - lw)
        beta = n * learn_all[:, s] * inv
        key = w * inv
        q = r * jnp.exp(lt)
        bonus_ref[:, s] = dot_exact_right(r * w * rw_ref[0:1, s], ones) * v
        qa2, q2 = two(qa), two(q)
        left = jnp.concatenate([qa2, q2], axis=0)
        right = jnp.concatenate([beta, beta, key, key], axis=0)
        grams.append(dot3(left, right, NT))
        qas.append(qa2)
        qs.append(q2)
        betas.append(two(beta))
        keys.append(two(key))
        vvs.append(two(v))
        growths.append(lt)
    mixes = [jnp.where(strict, g[:PAIR, :PAIR], 0.0) for g in grams]
    inverses = [eye + jnp.where(row // 2 == col // 2, m, 0.0) for m in mixes]
    b = 2
    while b < CHUNK:
        off = (row // (2 * b) == col // (2 * b)) & (row // b != col // b)
        inner = [dot3(jnp.where(off, m, 0.0), x) for m, x in zip(mixes, inverses)]
        inverses = [x + dot3(x, i) for x, i in zip(inverses, inner)]
        b *= 2
    for p, s in enumerate(sides):
        g = grams[p]
        mix_key = jnp.where(strict, g[:PAIR, PAIR:], 0.0)
        read_beta = jnp.where(diag, g[PAIR:, :PAIR], 0.0)
        read_key = jnp.where(diag, g[PAIR:, PAIR:], 0.0)
        kv = dot3(jnp.concatenate([mix_key, read_key], axis=0), vvs[p])
        uw = dot3(
            inverses[p], jnp.concatenate([kv[:PAIR], qas[p] * from_start], axis=1)
        )
        rb = dot3(read_beta, uw)
        z_ref[:, s] = fold(rb[:, :PAIR] + kv[PAIR:])
        y_ref[:, s] = fold(rb[:, PAIR:] + qs[p] * from_start)
        u, w = uw[:, :PAIR], uw[:, PAIR:]
        earlier = run_ref[p]

        def maps(weight, growth, kept):
            bw = betas[p] * (weight * growth)
            kw = keys[p] * (weight * growth)
            both = dot3(uw, bw, TN)
            extra = dot3(vvs[p], kw, TN)
            return both[PAIR:] + eye * (growth * kept), both[:PAIR] + extra

        growth = jnp.exp(growths[p][CHUNK - 1 : CHUNK])
        a_map, b_map = maps(chosen, growth, keep)
        a_ref[0, p] = a_map
        b_ref[0, p] = b_map
        later = dot3(earlier, a_map)
        run_ref[p] = later + jnp.concatenate([jnp.zeros_like(b_map), b_map], axis=0)

        @pl.when(inside == 1)
        def _():
            step = jnp.where(row < CHUNK, row, row - CHUNK)
            here = ((epc2 == e_end) & (step <= moment)).astype(F32)
            pick = lax.broadcasted_iota(jnp.int32, (CHUNK, PAIR), 0) == moment
            grow = jnp.exp(jnp.sum(jnp.where(pick, growths[p], 0.0), axis=0, keepdims=True))
            kept = jnp.where(e_end == e_in, 1.0, 0.0).astype(F32)
            a_end, b_end = maps(here, grow, kept)
            ended = dot3(earlier, a_end)
            maps_ref[0, p] = fold(ended[:PAIR]).astype(BF16)
            maps_ref[2, p] = fold(ended[PAIR:] + b_end).astype(BF16)

        @pl.when(c == pl.num_programs(0) - 1)
        def _():
            maps_ref[1, p] = fold(run_ref[p, PAIR:]).astype(BF16)

        @pl.when((c == pl.num_programs(0) - 1) & (scal_ref[c, 5] == 0))
        def _():
            maps_ref[0, p] = fold(run_ref[p, :PAIR]).astype(BF16)


def read_kernel(
    scal_ref, all_ref, y_ref, z_ref, bonus_ref, gate_ref, gain_ref, a_ref, b_ref,
    vis_ref, final_ref, state_ref, mine_ref,
):
    c = pl.program_id(0)
    pairs = y_ref.shape[1] // PAIR
    count = all_ref.shape[0]
    position = scal_ref[0]

    @pl.when(c == 0)
    def _():
        final_ref[...] = jnp.zeros_like(final_ref)
        state_ref[...] = jnp.zeros_like(state_ref)

        def hop(d, carry):
            @pl.when(d == position)
            def _():
                mine_ref[...] = state_ref[...]

            holds = (d == scal_ref[1]) | (d == scal_ref[2])
            owner = jnp.where(d == scal_ref[1], scal_ref[3], scal_ref[4])

            for p in range(pairs):
                state = state_ref[p]
                high, low = split(state)
                a_map = two(all_ref[d, 0, p].astype(F32)).astype(BF16)
                moved = lax.dot_general(high, a_map, NN, preferred_element_type=F32)
                moved = moved + lax.dot_general(low, a_map, NN, preferred_element_type=F32)

                @pl.when(holds & (owner == position))
                def _():
                    final_ref[p] = fold(moved) + all_ref[d, 2, p].astype(F32)

                local = two(all_ref[d, 1, p].astype(F32))
                state_ref[p] = jnp.where(holds, 0.0, moved) + local
            return carry

        lax.fori_loop(0, count, hop, 0)

    ones = head_ones()
    for p in range(pairs):
        s = slice(p * PAIR, (p + 1) * PAIR)
        state = mine_ref[p]
        out = fold(dot3(two(y_ref[:, s]), state, NT)) + z_ref[:, s]
        mine_ref[p] = dot3(state, a_ref[0, p]) + b_ref[0, p]
        centre = out - dot_exact_right(out, ones) * (1.0 / HEAD)
        spread = dot_exact_right(centre * centre, ones) * (1.0 / HEAD)
        normed = centre * lax.rsqrt(spread + GROUP_EPS) * gain_ref[0:1, s]
        vis_ref[:, s] = ((normed + bonus_ref[:, s]) * gate_ref[:, s]).astype(BF16)


def from_behind(array, axis, by):
    length = lax.axis_size(axis)
    pairs = [(i, i + by) for i in range(length) if 0 <= i + by < length]
    return lax.ppermute(array, axis, pairs)


def matmul(left, right):
    return jnp.dot(left, right, preferred_element_type=F32)


def on_device(
    layer_activation,
    sequence_label,
    sequence_extents,
    destination_slots,
    entry_layernorm_coef,
    lagged_blend_coefs,
    query_matrix,
    lookup_matrix,
    content_matrix,
    readout_matrix,
    forgetting_narrow_matrix,
    forgetting_widen_matrix,
    forgetting_offset,
    stepsize_narrow_matrix,
    stepsize_widen_matrix,
    stepsize_offset,
    gating_narrow_matrix,
    gating_widen_matrix,
    erasure_lookup_coef,
    lookup_step_fraction,
    diagonal_reward_coef,
    group_layernorm_coef,
):
    tokens = layer_activation.shape[0]
    width = query_matrix.shape[1]
    pairs = width // PAIR
    chunks = tokens // CHUNK
    position = lax.axis_index("seq")
    column = lax.axis_index("tp")
    n_seq = lax.axis_size("seq")
    gathered = lax.all_gather(layer_activation, "tp", axis=1, tiled=True)
    floats = gathered.astype(F32)
    average = jnp.mean(floats, axis=1, keepdims=True)
    centred = floats - average
    variance = jnp.mean(centred * centred, axis=1, keepdims=True)
    normed = (centred * lax.rsqrt(variance + EPS) * entry_layernorm_coef).astype(BF16)
    normal_f = normed.astype(F32)
    arrived = from_behind(normed[-1:], "seq", 1)
    bounds = jnp.cumsum(sequence_extents)
    first_token = position * tokens
    before = first_token - 1
    segment_before = (before >= bounds[0]).astype(jnp.int32) + (before >= bounds[1]).astype(
        jnp.int32
    )
    joined = (segment_before == sequence_label[0]) & (position > 0)
    continues = jnp.concatenate([joined[None], sequence_label[1:] == sequence_label[:-1]])
    previous = jnp.concatenate([arrived.astype(F32), normal_f[:-1]], axis=0)
    previous = jnp.where(continues[:, None], previous, jnp.zeros_like(previous))
    difference = previous - normal_f

    def blended(which):
        return (normal_f + difference * lagged_blend_coefs[which]).astype(BF16)

    receptance = matmul(blended(0), query_matrix)
    keys = matmul(blended(2), lookup_matrix)
    values = matmul(blended(3), content_matrix)
    decay_hidden = jnp.tanh(matmul(blended(1), forgetting_narrow_matrix)).astype(BF16)
    learn_hidden = matmul(blended(4), stepsize_narrow_matrix).astype(BF16)
    gate_hidden = jax.nn.sigmoid(matmul(blended(5), gating_narrow_matrix)).astype(BF16)
    forget_logit = forgetting_offset + matmul(decay_hidden, forgetting_widen_matrix)
    learn_logit = stepsize_offset + matmul(learn_hidden, stepsize_widen_matrix)
    gating_signal = matmul(gate_hidden, gating_widen_matrix)

    ends = bounds - 1
    holders = ends // tokens
    epochs = segment_before + jnp.zeros((tokens,), jnp.int32)
    epochs = sequence_label
    before_first = jnp.where(position > 0, segment_before, -1)
    grouped = epochs.reshape(chunks, CHUNK)
    e_last = grouped[:, -1]
    e_in = jnp.concatenate([before_first[None], e_last[:-1]])
    starts = first_token + jnp.arange(chunks, dtype=jnp.int32) * CHUNK
    offsets = ends[None, :] - starts[:, None]
    within = (offsets >= 0) & (offsets < CHUNK)
    inside = jnp.any(within, axis=1).astype(jnp.int32)
    moment = jnp.sum(jnp.where(within, offsets, 0), axis=1)
    e_end = jnp.sum(jnp.where(within, jnp.arange(PROMPTS, dtype=jnp.int32)[None], 0), axis=1)
    device_ends = jnp.broadcast_to(jnp.any(holders == position).astype(jnp.int32), (chunks,))
    scalars = jnp.stack([e_in, e_last, inside, moment, e_end, device_ends], axis=1)
    ep_cols = jnp.broadcast_to(epochs[:, None], (tokens, PAIR))
    ep_rows = jnp.broadcast_to(
        jnp.concatenate([grouped, grouped], axis=1)[:, None, :], (chunks, 8, PAIR)
    )

    def wide():
        return pl.BlockSpec((CHUNK, width), lambda c: (c, 0))

    def coef():
        return pl.BlockSpec((1, width), lambda c: (0, 0))

    def mats():
        return pl.BlockSpec((1, pairs, PAIR, PAIR), lambda c: (c, 0, 0, 0))

    smem = pl.BlockSpec(memory_space=pltpu.SMEM)
    big = jax.ShapeDtypeStruct((tokens, width), F32)
    mat = jax.ShapeDtypeStruct((chunks, pairs, PAIR, PAIR), F32)
    y, z, bonus, a_maps, b_maps, maps = pl.pallas_call(
        chunk_kernel,
        grid=(chunks,),
        in_specs=[smem]
        + [wide()] * 5
        + [coef()] * 3
        + [
            pl.BlockSpec((CHUNK, PAIR), lambda c: (c, 0)),
            pl.BlockSpec((1, 8, PAIR), lambda c: (c, 0, 0)),
        ],
        out_specs=[
            wide(),
            wide(),
            wide(),
            mats(),
            mats(),
            pl.BlockSpec((3, pairs, HEAD, PAIR), lambda c: (0, 0, 0, 0)),
        ],
        out_shape=[big, big, big, mat, mat, jax.ShapeDtypeStruct((3, pairs, HEAD, PAIR), BF16)],
        scratch_shapes=[pltpu.VMEM((pairs, 2 * PAIR, PAIR), F32)],
        compiler_params=pltpu.CompilerParams(vmem_limit_bytes=40 << 20),
    )(
        scalars,
        receptance,
        keys,
        values,
        forget_logit,
        learn_logit,
        erasure_lookup_coef[None],
        lookup_step_fraction[None],
        diagonal_reward_coef[None],
        ep_cols,
        ep_rows,
    )

    local_end = jnp.clip(jnp.max(jnp.where(holders == position, ends - first_token, 0)), 0, tokens - 1)
    row_end = lax.dynamic_slice(normed, (local_end, column * width), (1, width))
    sent = jnp.concatenate(
        [
            maps.reshape(3 * pairs * HEAD, PAIR),
            jnp.pad(row_end.reshape(pairs, PAIR), ((0, 16 - pairs), (0, 0))),
        ],
        axis=0,
    )
    everyone = lax.all_gather(sent, "seq", axis=0, tiled=False)
    all_maps = everyone[:, : 3 * pairs * HEAD].reshape(n_seq, 3, pairs, HEAD, PAIR)
    rows = everyone[:, 3 * pairs * HEAD : 3 * pairs * HEAD + pairs].reshape(n_seq, width)

    facts = jnp.concatenate([position[None], holders, destination_slots]).astype(jnp.int32)
    visible, final_fold = pl.pallas_call(
        read_kernel,
        grid=(chunks,),
        in_specs=[
            smem,
            pl.BlockSpec((n_seq, 3, pairs, HEAD, PAIR), lambda c: (0, 0, 0, 0, 0), pipeline_mode=pl.Buffered(1)),
            wide(),
            wide(),
            wide(),
            wide(),
            coef(),
            mats(),
            mats(),
        ],
        out_specs=[wide(), pl.BlockSpec((pairs, HEAD, PAIR), lambda c: (0, 0, 0))],
        out_shape=[
            jax.ShapeDtypeStruct((tokens, width), BF16),
            jax.ShapeDtypeStruct((pairs, HEAD, PAIR), F32),
        ],
        scratch_shapes=[pltpu.VMEM((pairs, PAIR, PAIR), F32), pltpu.VMEM((pairs, PAIR, PAIR), F32)],
        compiler_params=pltpu.CompilerParams(vmem_limit_bytes=48 << 20),
    )(facts, all_maps, y, z, bonus, gating_signal, group_layernorm_coef[None], a_maps, b_maps)

    final_states = final_fold.reshape(pairs, HEAD, 2, HEAD).transpose(0, 2, 1, 3)
    final_states = final_states.reshape(1, 2 * pairs, HEAD, HEAD)
    final_rows = jnp.zeros((1, width), BF16)
    for prompt in range(PROMPTS):
        got = lax.dynamic_slice(rows, (holders[prompt], 0), (1, width))
        final_rows = jnp.where(position == destination_slots[prompt], got, final_rows)

    partial_value = matmul(visible, readout_matrix)
    summed = lax.psum_scatter(
        partial_value.astype(BF16), "tp", scatter_dimension=1, tiled=True
    ).astype(F32)
    mixed = (summed + layer_activation.astype(F32)).astype(BF16)
    return (mixed, final_states, final_rows)


def solution(mesh):
    return jax.shard_map(
        on_device,
        mesh=mesh,
        in_specs=(
            P("seq", "tp"),
            P("seq"),
            P(),
            P(),
            P(),
            P(),
            P(None, "tp"),
            P(None, "tp"),
            P(None, "tp"),
            P("tp", None),
            P(),
            P(None, "tp"),
            P("tp"),
            P(),
            P(None, "tp"),
            P("tp"),
            P(),
            P(None, "tp"),
            P("tp"),
            P("tp"),
            P("tp"),
            P("tp"),
        ),
        out_specs=(P("seq", "tp"), P("seq", "tp", None, None), P("seq", "tp")),
        check_vma=False,
    )
```

time: 701 us -> 212 us (0.30)
  other arithmetic: 299 us -> 10.9 us
  matrix products: 120 us -> 22.5 us
  Pallas kernels: 0 us -> 55.2 us
  local copies, waits for them, and re-layouts: 62.6 us -> 23.2 us
  waiting for transfers between devices: 109 us -> 73.6 us
  starting transfers between devices: 36.9 us -> 3.68 us
  loops' own time: 29.5 us -> 0 us
  blocking collectives: 22.7 us -> 0 us
    another operation x31 -> x2, other arithmetic: 257 us -> 0.9 us  [the longest x18 245 us: block_step(): jax.scipy.linalg.solve_triangular(unit_eye[None] - mix_beta, right_side,...]
    dot_general x107 -> x7, matrix products: 110 us -> 22.5 us  [matmul(): return jnp.dot(left, right, preferred_element_type=F32)]
    pallas_call x0 -> x2, Pallas kernels: none -> 55.2 us  [the longest x1 38.7 us: on_device(): pl.pallas_call(chunk_kernel, grid=(chunks,), in_specs=[smem] + [wide()] *...]
    psum x1 -> x0, waiting for transfers between devices: 43.6 us -> none  [broadcast(): return lax.psum(kept, axis)]
    all_gather x0 -> x1, waiting for transfers between devices: none -> 39.5 us  [on_device(): everyone = lax.all_gather(sent, 'seq', axis=0, tiled=False)]
    ppermute x8 -> x1, starting transfers between devices: 36.8 us -> 3.38 us  [from_behind(): return lax.ppermute(array, axis, pairs)]
    another operation x2 -> x0, loops' own time: 29.5 us -> none  [the longest x1 29.1 us: on_device(): lax.scan(block_step, (start_stack, start_saved), scan_inputs)]
    psum x1 -> x0, blocking collectives: 22.7 us -> none  [broadcast(): return lax.psum(kept, axis)]
  transfers between devices with their start and end apart: 11 -> 4, of which waited for: 10 -> 3; matrix products, arithmetic and copies ran while one was open for 2% -> 9% of each run, Pallas kernels for 0% -> 0%
where the time goes in v1:
time: 212 us; the launch traced here: 211 us
  waiting for transfers between devices  73.6 us (35%)
  Pallas kernels  55.2 us (26%)
  local copies, waits for them, and re-layouts  23.2 us (11%)
  matrix products  22.5 us (11%)
  between operations  22.4 us (11%)
  other arithmetic  10.9 us (5%)
  starting transfers between devices  3.68 us (2%)
    all_gather x1, waiting for transfers between devices, on_device(): everyone = lax.all_gather(sent, 'seq', axis=0, tiled=False)  39.5 us
    pallas_call x1, Pallas kernels, on_device(): pl.pallas_call(chunk_kernel, grid=(chunks,), in_specs=[smem] + [wide()] *...  38.7 us
    dot_general x7, matrix products, matmul(): return jnp.dot(left, right, preferred_element_type=F32)  22.5 us
    reduce_scatter x1, waiting for transfers between devices, on_device(): lax.psum_scatter(partial_value.astype(BF16), 'tp', scatter_dimension=1, t...  18.7 us
    pallas_call x1, Pallas kernels, on_device(): pl.pallas_call(read_kernel, grid=(chunks,), in_specs=[smem, pl.BlockSpec(...  16.5 us
    all_gather x1, waiting for transfers between devices, on_device(): gathered = lax.all_gather(layer_activation, 'tp', axis=1, tiled=True)  14.8 us
    unnamed x70, local copies, waits for them, and re-layouts  12.8 us
  transfers between devices with their start and end apart: 4, of which 3 were waited for; matrix products, arithmetic and copies ran while one was open for 9% of the time, Pallas kernels for 0%

profile of v1, /device:TPU:0, one launch (start us, length us, event | category | flops | bytes accessed | tf_op | source)
XLA Modules:
  0.0 211.4 jit_solution(10410226493161843661)
XLA Ops:
  7.2 0.7 all-gather.4.cloned.1.call-update
  8.0 1.3 slice.74
  9.2 0.8 reshape.76
  10.0 0.8 reduce-window.4
  10.8 0.6 fusion.70
  13.4 0.8 slice_compare_fusion
  14.2 0.1 pad_add_fusion.1
  14.3 0.1 pad_add_fusion
  14.4 0.2 slice_reduce_fusion
  14.6 0.6 compare_reduce_fusion
  15.2 0.6 fusion.64
  15.9 0.1 fusion.66
  16.0 0.1 select_reduce_fusion
  16.0 1.1 fusion.67
  17.2 14.8 %all-gather.4.cloned.1.call-done = bf16[384,2048]{1,0:T(8,128)(2,1)} async-done(((bf16[384,512]{1,0:T(8,128)(2,1)}), bf16[384,2048]{1,0:T(8,128)(2,1)}) %all-gather.4.cloned.1.call-update) | async-done | bytes 1572880 | tf_op jit(solution)/shard_map/all_gather | solution.py:284
  32.0 1.8 convert_reduce_fusion
  33.8 2.0 fusion.2
  35.8 0.5 fusion.4
  36.3 1.2 copy-done.17
  37.5 3.4 %collective-permute-start = (bf16[1,2048]{1,0:T(2,128)(2,1)S(1)}, bf16[1,2048]{1,0:T(2,128)(2,1)S(1)}, u32[]{:S(2)}, u32[]{:S(2)}) collective-permute-start(bf16[1,2048]{1,0:T(2,128)(2,1)S(1)} %slice.91), channel_id=1, source_target_pairs={{0,4},{4,8},{8,12},{12,16},{16,20},{20,24},{24,28},{1,5},{5,9},{9,... | collective-permute-start | bytes 12296 | tf_op jit(solution)/shard_map/ppermute | solution.py:246
  40.9 0.1 add_bitcast_fusion
  42.4 0.1 copy.37
  42.5 0.1 copy.38
  42.6 0.1 copy.36
  42.7 0.1 copy.35
  42.8 0.1 stack.16.scal_ref
  42.8 1.9 slice.92
  44.8 0.1 dynamic-slice_reduce_fusion
  44.9 0.5 copy-done.25
  45.4 2.0 fusion.19.k_ref
  47.4 0.2 copy-done.26
  47.5 2.0 fusion.17.v_ref
  49.5 2.0 fusion.21.r_ref
  51.6 4.8 %convolution_add_fusion.1.fl_ref = f32[384,512]{1,0:T(8,128)} fusion(bf16[96,512]{1,0:T(8,128)(2,1)S(1)} %copy-done.30, bf16[2048,96]{0,1:T(8,128)(2,1)S(1)} %copy-done.28, bf16[384,2048]{1,0:T(8,128)(2,1)} %copy-done.17, f32[2048]{0:T(1024)S(1)} %bitcast.69, f32[512]{0:T(512)S(1)} %copy-done.32, f32[383,2048]{1,0:T(8,128)} %copy-done.20, ...), kind=kOutput, calls=%fused_computation.35 | convolution fusion | flops 194482176 | bytes 6007168 | tf_op jit(solution)/shard_map/dot_general | solution.py:250
  56.4 4.8 %convolution_add_fusion.ll_ref = f32[384,512]{1,0:T(8,128)} fusion(bf16[96,512]{1,0:T(8,128)(2,1)S(1)} %copy-done.31, bf16[2048,96]{0,1:T(8,128)(2,1)S(1)} %copy-done.29, bf16[384,2048]{1,0:T(8,128)(2,1)} %copy-done.17, f32[2048]{0:T(1024)S(1)} %bitcast.68, f32[512]{0:T(512)S(1)} %copy-done.33, f32[383,2048]{1,0:T(8,128)} %copy-done.20, ...), kind=kOutput, calls=%fused_computation.34 | convolution fusion | flops 194482176 | bytes 6007168 | tf_op jit(solution)/shard_map/dot_general | solution.py:250
  61.2 0.1 broadcast_in_dim.79.epc_ref
  61.3 1.1 copy-done.8
  62.5 1.1 copy-done.9
  63.6 1.1 copy-done.10
  64.7 1.1 copy-done.11
  65.9 1.1 copy-done.12
  67.0 38.7 %shard_map.229 = (f32[384,512]{1,0:T(8,128)S(1)}, f32[384,512]{1,0:T(8,128)S(1)}, f32[384,512]{1,0:T(8,128)S(1)}, f32[6,4,128,128]{3,2,1,0:T(8,128)S(1)}, f32[6,...) custom-call(s32[6,6]{1,0:T(8,128)S(1)} %stack.16.scal_ref, f32[384,512]{1,0:T(8,128)S(1)} %copy-done.10, ...), custom_call_target="tpu_custom_call" | custom-call | tf_op jit(solution)/shard_map/pallas_call | solution.py:350
  105.7 1.1 copy-done.1
  106.8 1.2 copy-done.2
  108.1 0.9 copy-done.3
  108.9 0.9 copy-done.5
  109.8 0.7 fusion.61
  110.5 0.2 reduce-scatter.2.cloned.1.call-start
  110.8 0.1 pad_add_fusion.2.scal_ref
  110.9 4.8 %fusion.45.gate_ref = f32[384,512]{1,0:T(8,128)} fusion(bf16[256,512]{1,0:T(8,128)(2,1)} %param.39, bf16[2048,256]{1,0:T(8,128)(2,1)} %param.38, bf16[384,2048]{1,0:T(8,128)(2,1)} %copy-done.17, f32[2048]{0:T(1024)S(1)} %bitcast.67, f32[383,2048]{1,0:T(8,128)} %copy-done.20, f32[1,2048]{1,0:T(1,128)S(1)} %convert_element_type.83, ...), kind=kOutput, calls=%fused_computation.41 | convolution fusion | flops 509214720 | bytes 6824320 | tf_op jit(solution)/shard_map/dot_general | solution.py:250
  115.6 39.5 %all-gather.6.cloned.1.call-done = bf16[6272,128]{1,0:T(8,128)(2,1)} async-done(((bf16[784,128]{1,0:T(8,128)(2,1)}), bf16[6272,128]{1,0:T(8,128)(2,1)}) %all-gather.6.cloned.1.call-update) | async-done | bytes 1605648 | tf_op jit(solution)/shard_map/all_gather | solution.py:394
  155.1 1.7 slice.93
  156.8 0.1 copy-done.6
  156.9 0.2 copy-done.7
  157.2 16.5 %shard_map.230 = (bf16[384,512]{1,0:T(8,128)(2,1)S(1)}, f32[4,64,128]{2,1,0:T(8,128)S(1)}) custom-call(s32[5]{0:T(128)S(1)} %pad_add_fusion.2.scal_ref, bf16[8,3,4,64,128]{4,3,2,1,0:T(8,128)(2,1)S(1)} %bitcast.56, f32[384,512]{1,0:T(8,128)S(1)} %get-tuple-element.12.y_ref, f32[384,512]{1,0:T(8,128)S(1)} %copy-done.4, f32[384,512]{1,0:T(8,128)S(1)} %copy-done.6, ...), custom_call_target="tpu_custom_call" | custom-call | tf_op jit(solution)/shard_map/pallas_call | solution.py:399
  173.7 2.2 %convolution_convert_fusion = bf16[384,2048]{1,0:T(8,128)(2,1)} fusion(bf16[384,512]{1,0:T(8,128)(2,1)S(1)} %get-tuple-element.17, bf16[512,2048]{1,0:T(8,128)(2,1)S(1)} %copy-done), kind=kOutput, calls=%fused_computation.21 | convolution fusion | flops 806092800 | bytes 4063232 | tf_op jit(solution)/shard_map/dot_general | solution.py:250
  175.9 0.6 fusion.68
  179.0 0.6 fusion.69
  182.1 0.7 slice_bitcast_fusion
  182.9 0.2 reshape.80
  183.1 0.7 copy.39
  183.8 0.6 broadcast_select_fusion.1
  184.4 18.7 %reduce-scatter.2.cloned.1.call-done = bf16[384,512]{1,0:T(8,128)(2,1)} async-done(((bf16[384,2048]{1,0:T(8,128)(2,1)}), bf16[384,512]{1,0:T(8,128)(2,1)}) %reduce-scatter.2.cloned.1.call-update) | async-done | bytes 393232 | tf_op jit(solution)/shard_map/reduce_scatter | solution.py:430
  203.1 1.8 add_convert_fusion
  (70 shorter events, 0.4 us)
Async XLA Ops:
  7.2 166.6 %copy-start = (bf16[512,2048]{1,0:T(8,128)(2,1)S(1)}, bf16[512,2048]{1,0:T(8,128)(2,1)}, u32[]{:S(2)}) copy-start(bf16[512,2048]{1,0:T(8,128)(2,1)} %param.31) | copy-start | bytes 6291460
  7.2 28.6 %copy-start.23 = (f32[2048]{0:T(1024)S(1)}, f32[2048]{0:T(1024)}, u32[]{:S(2)}) copy-start(f32[2048]{0:T(1024)} %param.26) | copy-start | bytes 24580
  7.2 24.8 %all-gather.4.cloned.1.call-start = ((), (), s32[]{:S(2)}) async-start(), calls=%async_computation.1 | async-start | bytes 1966080 | tf_op jit(solution)/shard_map/all_gather | solution.py:284
  7.9 147.2 %all-gather.6.cloned.1.call-start = ((), (), s32[]{:S(2)}) async-start(), calls=%async_computation.3 | async-start | bytes 1806336 | tf_op jit(solution)/shard_map/all_gather | solution.py:394
  32.0 3.8 %copy-start.19 = (bf16[384,2048]{1,0:T(8,128)(2,1)S(1)}, bf16[384,2048]{1,0:T(8,128)(2,1)}, u32[]{:S(2)}) copy-start(bf16[384,2048]{1,0:T(8,128)(2,1)} %all-gather.4.cloned.1.call-done) | copy-start | bytes 4718596
  36.3 1.2 copy-start.17
  37.5 7.4 %collective-permute-start = (bf16[1,2048]{1,0:T(2,128)(2,1)S(1)}, bf16[1,2048]{1,0:T(2,128)(2,1)S(1)}, u32[]{:S(2)}, u32[]{:S(2)}) collective-permute-start(bf16[1,2048]{1,0:T(2,128)(2,1)S(1)} %slice.91), channel_id=1, source_target_pairs={{0,4},{4,8},{8,12},{12,16},{16,20},{20,24},{24,28},{1,5},{5,9},{9,... | collective-permute-start | bytes 12296 | tf_op jit(solution)/shard_map/ppermute | solution.py:246
  42.8 1.9 copy-start.18
  42.8 2.5 %copy-start.25 = (bf16[2048,512]{1,0:T(8,128)(2,1)S(1)}, bf16[2048,512]{1,0:T(8,128)(2,1)}, u32[]{:S(2)}) copy-start(bf16[2048,512]{1,0:T(8,128)(2,1)} %param.29) | copy-start | bytes 6291460
  44.8 4.7 %copy-start.20 = (f32[383,2048]{1,0:T(8,128)}, f32[383,2048]{1,0:T(8,128)S(1)}, u32[]{:S(2)}) copy-start(f32[383,2048]{1,0:T(8,128)S(1)} %slice.92) | copy-start | bytes 9412612
  45.4 2.1 %copy-start.26 = (bf16[2048,512]{1,0:T(8,128)(2,1)S(1)}, bf16[2048,512]{1,0:T(8,128)(2,1)}, u32[]{:S(2)}) copy-start(bf16[2048,512]{1,0:T(8,128)(2,1)} %param.30) | copy-start | bytes 6291460
  47.5 2.0 copy-start.27
  49.5 2.0 copy-start.28
  49.5 2.0 copy-start.30
  49.5 2.0 copy-start.32
  51.6 4.8 %copy-start.29 = (bf16[2048,96]{0,1:T(8,128)(2,1)S(1)}, bf16[2048,96]{0,1:T(8,128)(2,1)}, u32[]{:S(2)}) copy-start(bf16[2048,96]{0,1:T(8,128)(2,1)} %param.35) | copy-start | bytes 1179652
  51.6 4.8 %copy-start.31 = (bf16[96,512]{1,0:T(8,128)(2,1)S(1)}, bf16[96,512]{1,0:T(8,128)(2,1)}, u32[]{:S(2)}) copy-start(bf16[96,512]{1,0:T(8,128)(2,1)} %param.36) | copy-start | bytes 294916
  51.6 4.8 %copy-start.33 = (f32[512]{0:T(512)S(1)}, f32[512]{0:T(512)}, u32[]{:S(2)}) copy-start(f32[512]{0:T(512)} %param.37) | copy-start | bytes 6148
  56.4 4.8 %copy-start.22 = (s32[384]{0:T(512)S(1)}, s32[384]{0:T(512)}, u32[]{:S(2)}) copy-start(s32[384]{0:T(512)} %param.23) | copy-start | bytes 4612
  56.4 4.9 %copy-start.13 = (f32[512]{0:T(512)S(1)}, f32[512]{0:T(512)}, u32[]{:S(2)}) copy-start(f32[512]{0:T(512)} %param.40) | copy-start | bytes 6148
  56.4 4.9 %copy-start.14 = (f32[512]{0:T(512)S(1)}, f32[512]{0:T(512)}, u32[]{:S(2)}) copy-start(f32[512]{0:T(512)} %param.41) | copy-start | bytes 6148
  56.4 4.9 %copy-start.15 = (f32[512]{0:T(512)S(1)}, f32[512]{0:T(512)}, u32[]{:S(2)}) copy-start(f32[512]{0:T(512)} %param.42) | copy-start | bytes 6148
  61.2 49.6 %copy-start.24 = (s32[2]{0:T(128)S(1)}, s32[2]{0:T(128)}, u32[]{:S(2)}) copy-start(s32[2]{0:T(128)} %param.25) | copy-start | bytes 28
  61.3 1.1 copy-start.8
  62.5 1.1 copy-start.9
  63.6 1.1 copy-start.10
  64.7 1.1 copy-start.11
  65.9 1.1 copy-start.12
  105.7 1.1 copy-start.1
  106.8 1.2 copy-start.2
  108.1 0.9 copy-start.3
  108.9 0.9 copy-start.5
  110.5 92.5 %reduce-scatter.2.cloned.1.call-start = ((), (), s32[]{:S(2)}) async-start(), calls=%async_computation.2 | async-start | bytes 1966080 | tf_op jit(solution)/shard_map/reduce_scatter | solution.py:430
  115.6 41.2 %copy-start.16 = (f32[512]{0:T(512)S(1)}, f32[512]{0:T(512)}, u32[]{:S(2)}) copy-start(f32[512]{0:T(512)} %param.43) | copy-start | bytes 6148
  155.1 1.7 copy-start.4
  155.1 1.8 copy-start.6
  155.1 2.1 copy-start.7
  173.7 29.3 %copy-start.21 = (bf16[384,512]{1,0:T(8,128)(2,1)S(1)}, bf16[384,512]{1,0:T(8,128)(2,1)}, u32[]{:S(2)}) copy-start(bf16[384,512]{1,0:T(8,128)(2,1)} %param.22) | copy-start | bytes 1179652
Sparse Core Ops, SparseCore 0:
  9.6 22.3 all-gather.3
  110.7 44.4 all-gather.5
  176.1 26.9 reduce-scatter.1

commit v2 on v1

v2 whole, which is shorter than its diff:
```python
import jax
import jax.numpy as jnp
from jax import lax
from jax.experimental import pallas as pl
from jax.experimental.pallas import tpu as pltpu
from jax.sharding import PartitionSpec as P

HEAD = 64
PAIR = 128
PROMPTS = 2
CHUNK = 64
SUBS = 2
EPS = 1e-05
GROUP_EPS = 0.00064
F32 = jnp.float32
BF16 = jnp.bfloat16
NN = (((1,), (0,)), ((), ()))
NT = (((1,), (1,)), ((), ()))
TN = (((0,), (0,)), ((), ()))


def split(x):
    high = x.astype(BF16)
    return high, (x - high.astype(F32)).astype(BF16)


def dot1(a, b, dims=NN):
    return lax.dot_general(a.astype(BF16), b.astype(BF16), dims, preferred_element_type=F32)


def dot3(a, b, dims=NN):
    (left,), (right,) = dims[0]
    ah, al = split(a)
    bh, bl = split(b)
    return lax.dot_general(
        jnp.concatenate([ah, al, ah], axis=left),
        jnp.concatenate([bh, bh, bl], axis=right),
        dims,
        preferred_element_type=F32,
    )


def dot_exact_right(a, b):
    ah, al = split(a)
    return lax.dot_general(
        jnp.concatenate([ah, al], axis=1),
        jnp.concatenate([b, b], axis=0),
        NN,
        preferred_element_type=F32,
    )


def head_ones():
    row = lax.broadcasted_iota(jnp.int32, (PAIR, PAIR), 0) // HEAD
    col = lax.broadcasted_iota(jnp.int32, (PAIR, PAIR), 1) // HEAD
    return (row == col).astype(BF16)


def two(x):
    lane = lax.broadcasted_iota(jnp.int32, x.shape, 1)
    zero = jnp.zeros_like(x)
    return jnp.concatenate(
        [jnp.where(lane < HEAD, x, zero), jnp.where(lane >= HEAD, x, zero)], axis=0
    )


def fold(x):
    return x[:HEAD] + x[HEAD:]


def rms_rows(x, coef):
    average = jnp.mean(x, axis=1, keepdims=True)
    centred = x - average
    variance = jnp.mean(centred * centred, axis=1, keepdims=True)
    return (centred * lax.rsqrt(variance + EPS) * coef).astype(BF16).astype(F32)


def project(
    x_ref, row_ref, cont_ref, ln_ref, mix_ref, wq_ref, wk_ref, wv_ref, fn_ref, fw_ref, fo_ref,
    sn_ref, sw_ref, so_ref, gn_ref, gw_ref, gate_ref, norm_ref, blend_ref, r_ref, k_ref, v_ref,
    fl_ref, ll_ref,
):
    tokens, features = x_ref.shape
    coef = ln_ref[0:1, :]
    first = jnp.broadcast_to(row_ref[0:1, :].astype(F32), (8, features))
    norm_ref[0:8, :] = rms_rows(first, coef)
    slab = 64
    block = 512

    def normalise(i, carry):
        rows = pl.ds(pl.multiple_of(i * slab, slab), slab)
        norm_ref[pl.ds(pl.multiple_of(8 + i * slab, 8), slab), :] = rms_rows(
            x_ref[rows, :].astype(F32), coef
        )
        return carry

    lax.fori_loop(0, tokens // slab, normalise, 0)
    for i in range(tokens // slab):
        cont = cont_ref[i * slab : (i + 1) * slab, 0:1] > 0.5
        for f in range(features // block):
            cols = slice(f * block, (f + 1) * block)
            here = norm_ref[8 + i * slab : 8 + (i + 1) * slab, cols]
            past = norm_ref[7 + i * slab : 7 + (i + 1) * slab, cols]
            gap = jnp.where(cont, past, 0.0) - here
            for w in range(6):
                blend_ref[w, i * slab : (i + 1) * slab, cols] = (
                    here + gap * mix_ref[w : w + 1, cols]
                ).astype(BF16)

    def mm(left, right):
        return jnp.dot(left, right, preferred_element_type=F32)

    r_ref[...] = mm(blend_ref[0], wq_ref[...])
    k_ref[...] = mm(blend_ref[2], wk_ref[...])
    v_ref[...] = mm(blend_ref[3], wv_ref[...])
    hidden = jnp.tanh(mm(blend_ref[1], fn_ref[...])).astype(BF16)
    fl_ref[...] = fo_ref[0:1, :] + mm(hidden, fw_ref[...])
    hidden = mm(blend_ref[4], sn_ref[...]).astype(BF16)
    ll_ref[...] = so_ref[0:1, :] + mm(hidden, sw_ref[...])
    hidden = jax.nn.sigmoid(mm(blend_ref[5], gn_ref[...])).astype(BF16)
    gate_ref[...] = mm(hidden, gw_ref[...])


def chunk_kernel(
    scal_ref, x_ref, row_ref, cont_ref, ln_ref, mix_ref, wq_ref, wk_ref, wv_ref, fn_ref, fw_ref,
    fo_ref, sn_ref, sw_ref, so_ref, gn_ref, gw_ref, er_ref, fr_ref, rw_ref, epc_ref, epr_ref,
    y_ref, z_ref, bonus_ref, a_ref, b_ref, maps_ref, gate_ref,
    run_ref, norm_ref, blend_ref, rs_ref, ks_ref, vs_ref, fl_ref, ll_ref,
):
    step = pl.program_id(0)
    last_step = pl.num_programs(0) - 1
    pairs = rs_ref.shape[1] // PAIR

    row = lax.broadcasted_iota(jnp.int32, (PAIR, PAIR), 0)
    col = lax.broadcasted_iota(jnp.int32, (PAIR, PAIR), 1)
    eye = (row == col).astype(F32)

    @pl.when(step == 0)
    def _():
        project(
            x_ref, row_ref, cont_ref, ln_ref, mix_ref, wq_ref, wk_ref, wv_ref, fn_ref, fw_ref,
            fo_ref, sn_ref, sw_ref, so_ref, gn_ref, gw_ref, gate_ref, norm_ref, blend_ref,
            rs_ref, ks_ref, vs_ref, fl_ref, ll_ref,
        )
        maps_ref[...] = jnp.zeros_like(maps_ref)
        for p in range(pairs):
            run_ref[p] = jnp.concatenate([eye, jnp.zeros_like(eye)], axis=0)

    ones = head_ones()
    tri = (
        lax.broadcasted_iota(jnp.int32, (CHUNK, CHUNK), 0)
        >= lax.broadcasted_iota(jnp.int32, (CHUNK, CHUNK), 1)
    ).astype(F32)
    sides = [slice(p * PAIR, (p + 1) * PAIR) for p in range(pairs)]
    items = []
    for sub in range(SUBS):
        c = step * SUBS + sub
        rows = pl.ds(pl.multiple_of(c * CHUNK, CHUNK), CHUNK)
        here = slice(sub * CHUNK, (sub + 1) * CHUNK)
        e_in, e_last = scal_ref[c, 0], scal_ref[c, 1]
        epc = epc_ref[here, :]
        epc2 = jnp.concatenate([epc, epc], axis=0)
        epr = epr_ref[sub, 0:1, :]
        same = (row // HEAD == col // HEAD) & (epc2 == epr)
        strict = same & (row > col)
        diag = same & (row >= col)
        from_start = (epc2 == e_in).astype(F32)
        chosen = (epc2 == e_last).astype(F32)
        keep = jnp.where(e_last == e_in, 1.0, 0.0).astype(F32)
        lw_all = -0.6065306597126334 * jax.nn.sigmoid(fl_ref[rows, :])
        lt_all = jnp.dot(tri, lw_all, precision=lax.Precision.HIGHEST, preferred_element_type=F32)
        learn_all = jax.nn.sigmoid(ll_ref[rows, :])
        for p, s in enumerate(sides):
            lw, lt, learn = lw_all[:, s], lt_all[:, s], learn_all[:, s]
            k, r, v = ks_ref[rows, s], rs_ref[rows, s], vs_ref[rows, s]
            kk = k * er_ref[0:1, s]
            n = kk * lax.rsqrt(dot_exact_right(kk * kk, ones) + 1e-06)
            w = k * (1.0 + (learn - 1.0) * fr_ref[0:1, s])
            inv = jnp.exp(-lt)
            beta = n * learn * inv
            key = w * inv
            bonus_ref[here, s] = dot_exact_right(r * w * rw_ref[0:1, s], ones) * v
            qa2, q2 = two(-n * jnp.exp(lt - lw)), two(r * jnp.exp(lt))
            right = jnp.concatenate([beta, beta, key, key], axis=0)
            mixed = dot3(qa2, right, NT)
            read = dot1(q2, right, NT)
            items.append(
                dict(
                    c=c, sub=sub, p=p, s=s, here=here, lt=lt, epc2=epc2, e_in=e_in,
                    start=from_start, chosen=chosen, keep=keep,
                    qa=qa2, q=q2, beta=two(beta), key=two(key), v=two(v),
                    mix=jnp.where(strict, mixed[:, :PAIR], 0.0),
                    mix_key=jnp.where(strict, mixed[:, PAIR:], 0.0),
                    read_beta=jnp.where(diag, read[:, :PAIR], 0.0),
                    read_key=jnp.where(diag, read[:, PAIR:], 0.0),
                )
            )
    mixes = [i["mix"] for i in items]
    inverses = [eye + jnp.where(row // 2 == col // 2, m, 0.0) for m in mixes]
    b = 2
    while b < CHUNK:
        off = (row // (2 * b) == col // (2 * b)) & (row // b != col // b)
        inner = [dot1(jnp.where(off, m, 0.0), x) for m, x in zip(mixes, inverses)]
        inverses = [x + dot1(x, i) for x, i in zip(inverses, inner)]
        b *= 2
    rests = [eye - x + dot3(m, x) for m, x in zip(mixes, inverses)]
    inverses = [x + dot1(x, i) for x, i in zip(inverses, rests)]
    kvs = [dot3(i["mix_key"], i["v"]) for i in items]
    uws = [
        dot3(x, jnp.concatenate([kv, i["qa"] * i["start"]], axis=1))
        for x, kv, i in zip(inverses, kvs, items)
    ]
    for uw, i in zip(uws, items):
        rb = dot1(i["read_beta"], uw)
        rk = dot1(i["read_key"], i["v"])
        z_ref[i["here"], i["s"]] = fold(rb[:, :PAIR] + rk)
        y_ref[i["here"], i["s"]] = fold(rb[:, PAIR:] + i["q"] * i["start"])

    def maps(uw, i, weight, growth, kept):
        bw = i["beta"] * (weight * growth)
        kw = i["key"] * (weight * growth)
        both = dot3(uw, bw, TN)
        extra = dot3(i["v"], kw, TN)
        return both[PAIR:] + eye * (growth * kept), both[:PAIR] + extra

    pieces = [
        maps(uw, i, i["chosen"], jnp.exp(i["lt"][CHUNK - 1 : CHUNK]), i["keep"])
        for uw, i in zip(uws, items)
    ]
    for uw, i, (a_map, b_map) in zip(uws, items, pieces):
        p, c, sub = i["p"], i["c"], i["sub"]
        earlier = run_ref[p]
        a_ref[sub, p] = a_map
        b_ref[sub, p] = b_map
        later = dot3(earlier, a_map)
        run_ref[p] = later + jnp.concatenate([jnp.zeros_like(b_map), b_map], axis=0)

        @pl.when(scal_ref[c, 2] == 1)
        def _(uw=uw, i=i, p=p, c=c, earlier=earlier):
            moment, e_end = scal_ref[c, 3], scal_ref[c, 4]
            place = jnp.where(row < CHUNK, row, row - CHUNK)
            here = ((i["epc2"] == e_end) & (place <= moment)).astype(F32)
            pick = lax.broadcasted_iota(jnp.int32, (CHUNK, PAIR), 0) == moment
            grow = jnp.exp(jnp.sum(jnp.where(pick, i["lt"], 0.0), axis=0, keepdims=True))
            kept = jnp.where(e_end == i["e_in"], 1.0, 0.0).astype(F32)
            a_end, b_end = maps(uw, i, here, grow, kept)
            ended = dot3(earlier, a_end)
            maps_ref[0, p] = fold(ended[:PAIR]).astype(BF16)
            maps_ref[2, p] = fold(ended[PAIR:] + b_end).astype(BF16)

    @pl.when(step == last_step)
    def _():
        for p in range(pairs):
            maps_ref[1, p] = fold(run_ref[p, PAIR:]).astype(BF16)

        @pl.when(scal_ref[0, 5] == 0)
        def _():
            for p in range(pairs):
                maps_ref[0, p] = fold(run_ref[p, :PAIR]).astype(BF16)


def read_kernel(
    scal_ref, all_ref, y_ref, z_ref, bonus_ref, gate_ref, gain_ref, a_ref, b_ref,
    vis_ref, final_ref, state_ref, mine_ref,
):
    c = pl.program_id(0)
    pairs = y_ref.shape[1] // PAIR
    count = all_ref.shape[0]
    position = scal_ref[0]

    @pl.when(c == 0)
    def _():
        final_ref[...] = jnp.zeros_like(final_ref)
        state_ref[...] = jnp.zeros_like(state_ref)

        def hop(d, carry):
            @pl.when(d == position)
            def _():
                mine_ref[...] = state_ref[...]

            holds = (d == scal_ref[1]) | (d == scal_ref[2])
            owner = jnp.where(d == scal_ref[1], scal_ref[3], scal_ref[4])

            for p in range(pairs):
                state = state_ref[p]
                high, low = split(state)
                a_map = two(all_ref[d, 0, p].astype(F32)).astype(BF16)
                moved = lax.dot_general(high, a_map, NN, preferred_element_type=F32)
                moved = moved + lax.dot_general(low, a_map, NN, preferred_element_type=F32)

                @pl.when(holds & (owner == position))
                def _():
                    final_ref[p] = fold(moved) + all_ref[d, 2, p].astype(F32)

                local = two(all_ref[d, 1, p].astype(F32))
                state_ref[p] = jnp.where(holds, 0.0, moved) + local
            return carry

        lax.fori_loop(0, count, hop, 0)

    ones = head_ones()
    for p in range(pairs):
        s = slice(p * PAIR, (p + 1) * PAIR)
        state = mine_ref[p]
        out = fold(dot1(two(y_ref[:, s]), state, NT)) + z_ref[:, s]
        mine_ref[p] = dot3(state, a_ref[0, p]) + b_ref[0, p]
        centre = out - dot_exact_right(out, ones) * (1.0 / HEAD)
        spread = dot_exact_right(centre * centre, ones) * (1.0 / HEAD)
        normed = centre * lax.rsqrt(spread + GROUP_EPS) * gain_ref[0:1, s]
        vis_ref[:, s] = ((normed + bonus_ref[:, s]) * gate_ref[:, s]).astype(BF16)


def from_behind(array, axis, by):
    length = lax.axis_size(axis)
    pairs = [(i, i + by) for i in range(length) if 0 <= i + by < length]
    return lax.ppermute(array, axis, pairs)


def on_device(
    layer_activation,
    sequence_label,
    sequence_extents,
    destination_slots,
    entry_layernorm_coef,
    lagged_blend_coefs,
    query_matrix,
    lookup_matrix,
    content_matrix,
    readout_matrix,
    forgetting_narrow_matrix,
    forgetting_widen_matrix,
    forgetting_offset,
    stepsize_narrow_matrix,
    stepsize_widen_matrix,
    stepsize_offset,
    gating_narrow_matrix,
    gating_widen_matrix,
    erasure_lookup_coef,
    lookup_step_fraction,
    diagonal_reward_coef,
    group_layernorm_coef,
):
    tokens = layer_activation.shape[0]
    width = query_matrix.shape[1]
    pairs = width // PAIR
    chunks = tokens // CHUNK
    position = lax.axis_index("seq")
    column = lax.axis_index("tp")
    n_seq = lax.axis_size("seq")
    gathered = lax.all_gather(layer_activation, "tp", axis=1, tiled=True)
    arrived = from_behind(gathered[-1:], "seq", 1)
    bounds = jnp.cumsum(sequence_extents)
    first_token = position * tokens
    before = first_token - 1
    segment_before = (before >= bounds[0]).astype(jnp.int32) + (before >= bounds[1]).astype(
        jnp.int32
    )
    joined = (segment_before == sequence_label[0]) & (position > 0)
    continues = jnp.concatenate([joined[None], sequence_label[1:] == sequence_label[:-1]])
    ends = bounds - 1
    holders = ends // tokens
    epochs = sequence_label
    before_first = jnp.where(position > 0, segment_before, -1)
    grouped = epochs.reshape(chunks, CHUNK)
    e_last = grouped[:, -1]
    e_in = jnp.concatenate([before_first[None], e_last[:-1]])
    starts = first_token + jnp.arange(chunks, dtype=jnp.int32) * CHUNK
    offsets = ends[None, :] - starts[:, None]
    within = (offsets >= 0) & (offsets < CHUNK)
    inside = jnp.any(within, axis=1).astype(jnp.int32)
    moment = jnp.sum(jnp.where(within, offsets, 0), axis=1)
    e_end = jnp.sum(jnp.where(within, jnp.arange(PROMPTS, dtype=jnp.int32)[None], 0), axis=1)
    device_ends = jnp.broadcast_to(jnp.any(holders == position).astype(jnp.int32), (chunks,))
    scalars = jnp.stack([e_in, e_last, inside, moment, e_end, device_ends], axis=1)
    ep_cols = jnp.broadcast_to(epochs[:, None], (tokens, PAIR))
    ep_rows = jnp.broadcast_to(
        jnp.concatenate([grouped, grouped], axis=1)[:, None, :], (chunks, 8, PAIR)
    )

    rows_per_step = CHUNK * SUBS

    def wide():
        return pl.BlockSpec((rows_per_step, width), lambda c: (c, 0))

    def tall():
        return pl.BlockSpec((CHUNK, width), lambda c: (c, 0))

    def coef():
        return pl.BlockSpec((1, width), lambda c: (0, 0))

    def whole(array):
        return pl.BlockSpec(array.shape, lambda c: (0,) * array.ndim, pipeline_mode=pl.Buffered(1))

    def mats(many):
        return pl.BlockSpec((many, pairs, PAIR, PAIR), lambda c: (c, 0, 0, 0))

    smem = pl.BlockSpec(memory_space=pltpu.SMEM)
    big = jax.ShapeDtypeStruct((tokens, width), F32)
    mat = jax.ShapeDtypeStruct((chunks, pairs, PAIR, PAIR), F32)
    fixed = [
        gathered,
        arrived,
        jnp.broadcast_to(continues.astype(F32)[:, None], (tokens, PAIR)),
        entry_layernorm_coef[None],
        lagged_blend_coefs,
        query_matrix,
        lookup_matrix,
        content_matrix,
        forgetting_narrow_matrix,
        forgetting_widen_matrix,
        forgetting_offset[None],
        stepsize_narrow_matrix,
        stepsize_widen_matrix,
        stepsize_offset[None],
        gating_narrow_matrix,
        gating_widen_matrix,
        erasure_lookup_coef[None],
        lookup_step_fraction[None],
        diagonal_reward_coef[None],
    ]
    features = gathered.shape[1]
    y, z, bonus, a_maps, b_maps, maps, gating_signal = pl.pallas_call(
        chunk_kernel,
        grid=(chunks // SUBS,),
        in_specs=[smem]
        + [whole(array) for array in fixed]
        + [
            pl.BlockSpec((rows_per_step, PAIR), lambda c: (c, 0)),
            pl.BlockSpec((SUBS, 8, PAIR), lambda c: (c, 0, 0)),
        ],
        out_specs=[
            wide(),
            wide(),
            wide(),
            mats(SUBS),
            mats(SUBS),
            pl.BlockSpec((3, pairs, HEAD, PAIR), lambda c: (0, 0, 0, 0)),
            pl.BlockSpec((tokens, width), lambda c: (0, 0)),
        ],
        out_shape=[
            big,
            big,
            big,
            mat,
            mat,
            jax.ShapeDtypeStruct((3, pairs, HEAD, PAIR), BF16),
            big,
        ],
        scratch_shapes=[
            pltpu.VMEM((pairs, 2 * PAIR, PAIR), F32),
            pltpu.VMEM((tokens + 8, features), F32),
            pltpu.VMEM((6, tokens, features), BF16),
        ]
        + [pltpu.VMEM((tokens, width), F32)] * 5,
        compiler_params=pltpu.CompilerParams(vmem_limit_bytes=56 << 20),
    )(scalars, *fixed, ep_cols, ep_rows)

    local_end = jnp.clip(jnp.max(jnp.where(holders == position, ends - first_token, 0)), 0, tokens - 1)
    row_raw = lax.dynamic_slice(gathered, (local_end, 0), (1, features)).astype(F32)
    row_norm = rms_rows(row_raw, entry_layernorm_coef).astype(BF16)
    row_end = lax.dynamic_slice(row_norm, (0, column * width), (1, width))
    sent = jnp.concatenate(
        [
            maps.reshape(3 * pairs * HEAD, PAIR),
            jnp.pad(row_end.reshape(pairs, PAIR), ((0, 16 - pairs), (0, 0))),
        ],
        axis=0,
    )
    everyone = lax.all_gather(sent, "seq", axis=0, tiled=False)
    all_maps = everyone[:, : 3 * pairs * HEAD].reshape(n_seq, 3, pairs, HEAD, PAIR)
    rows = everyone[:, 3 * pairs * HEAD : 3 * pairs * HEAD + pairs].reshape(n_seq, width)

    facts = jnp.concatenate([position[None], holders, destination_slots]).astype(jnp.int32)
    visible, final_fold = pl.pallas_call(
        read_kernel,
        grid=(chunks,),
        in_specs=[
            smem,
            pl.BlockSpec((n_seq, 3, pairs, HEAD, PAIR), lambda c: (0, 0, 0, 0, 0), pipeline_mode=pl.Buffered(1)),
            tall(),
            tall(),
            tall(),
            tall(),
            coef(),
            mats(1),
            mats(1),
        ],
        out_specs=[tall(), pl.BlockSpec((pairs, HEAD, PAIR), lambda c: (0, 0, 0))],
        out_shape=[
            jax.ShapeDtypeStruct((tokens, width), BF16),
            jax.ShapeDtypeStruct((pairs, HEAD, PAIR), F32),
        ],
        scratch_shapes=[pltpu.VMEM((pairs, PAIR, PAIR), F32), pltpu.VMEM((pairs, PAIR, PAIR), F32)],
        compiler_params=pltpu.CompilerParams(vmem_limit_bytes=48 << 20),
    )(facts, all_maps, y, z, bonus, gating_signal, group_layernorm_coef[None], a_maps, b_maps)

    final_states = final_fold.reshape(pairs, HEAD, 2, HEAD).transpose(0, 2, 1, 3)
    final_states = final_states.reshape(1, 2 * pairs, HEAD, HEAD)
    final_rows = jnp.zeros((1, width), BF16)
    for prompt in range(PROMPTS):
        got = lax.dynamic_slice(rows, (holders[prompt], 0), (1, width))
        final_rows = jnp.where(position == destination_slots[prompt], got, final_rows)

    partial_value = jnp.dot(visible, readout_matrix, preferred_element_type=F32)
    summed = lax.psum_scatter(
        partial_value.astype(BF16), "tp", scatter_dimension=1, tiled=True
    ).astype(F32)
    mixed = (summed + layer_activation.astype(F32)).astype(BF16)
    return (mixed, final_states, final_rows)


def solution(mesh):
    return jax.shard_map(
        on_device,
        mesh=mesh,
        in_specs=(
            P("seq", "tp"),
            P("seq"),
            P(),
            P(),
            P(),
            P(),
            P(None, "tp"),
            P(None, "tp"),
            P(None, "tp"),
            P("tp", None),
            P(),
            P(None, "tp"),
            P("tp"),
            P(),
            P(None, "tp"),
            P("tp"),
            P(),
            P(None, "tp"),
            P("tp"),
            P("tp"),
            P("tp"),
            P("tp"),
        ),
        out_specs=(P("seq", "tp"), P("seq", "tp", None, None), P("seq", "tp")),
        check_vma=False,
    )
```

time: 212 us -> 176 us (0.83)
  matrix products: 22.5 us -> 2.14 us
  Pallas kernels: 55.2 us -> 46.2 us
  local copies, waits for them, and re-layouts: 23.2 us -> 14.8 us
    dot_general x7 -> x1, matrix products: 22.5 us -> 2.14 us  [on_device(): partial_value = jnp.dot(visible, readout_matrix, preferred_element_type=F32)]
    unnamed x70 -> x26, local copies, waits for them, and re-layouts: 12.8 us -> 4.24 us
    pallas_call x1, Pallas kernels: 38.7 us -> 33.7 us  [on_device(): pl.pallas_call(chunk_kernel, grid=(chunks // SUBS,), in_specs=[smem] + [w...]
    all_gather x1, waiting for transfers between devices: 39.5 us -> 44 us  [on_device(): everyone = lax.all_gather(sent, 'seq', axis=0, tiled=False)]
    pallas_call x1, Pallas kernels: 16.5 us -> 12.5 us  [on_device(): pl.pallas_call(read_kernel, grid=(chunks,), in_specs=[smem, pl.BlockSpec(...]
    all_gather x1, waiting for transfers between devices: 14.8 us -> 11.2 us  [on_device(): gathered = lax.all_gather(layer_activation, 'tp', axis=1, tiled=True)]
    slice x3 -> x1, local copies, waits for them, and re-layouts: 3.08 us -> 0.77 us  [on_device(): arrived = from_behind(gathered[-1:], 'seq', 1)]
where the time goes in v2:
time: 176 us; the launch traced here: 175 us
  waiting for transfers between devices  74.8 us (42%)
  Pallas kernels  46.2 us (26%)
  between operations  23.3 us (13%)
  local copies, waits for them, and re-layouts  14.8 us (8%)
  other arithmetic  10.2 us (6%)
  starting transfers between devices  3.5 us (2%)
  matrix products  2.14 us (1%)
    all_gather x1, waiting for transfers between devices, on_device(): everyone = lax.all_gather(sent, 'seq', axis=0, tiled=False)  44 us
    pallas_call x1, Pallas kernels, on_device(): pl.pallas_call(chunk_kernel, grid=(chunks // SUBS,), in_specs=[smem] + [w...  33.7 us
    reduce_scatter x1, waiting for transfers between devices, on_device(): lax.psum_scatter(partial_value.astype(BF16), 'tp', scatter_dimension=1, t...  18.9 us
    pallas_call x1, Pallas kernels, on_device(): pl.pallas_call(read_kernel, grid=(chunks,), in_specs=[smem, pl.BlockSpec(...  12.5 us
    all_gather x1, waiting for transfers between devices, on_device(): gathered = lax.all_gather(layer_activation, 'tp', axis=1, tiled=True)  11.2 us
    unnamed x26, local copies, waits for them, and re-layouts  4.24 us
  transfers between devices with their start and end apart: 4, of which 3 were waited for; matrix products, arithmetic and copies ran while one was open for 9% of the time, Pallas kernels for 0%

profile of v2, /device:TPU:0, one launch (start us, length us, event | category | flops | bytes accessed | tf_op | source)
XLA Modules:
  0.0 175.0 jit_solution(13148140535625725395)
XLA Ops:
  7.2 0.0 copy-start
  7.2 0.0 copy-start.8
  7.2 0.0 copy-start.7
  7.2 0.0 all-gather.4.cloned.1.call-start
  7.2 0.7 all-gather.4.cloned.1.call-update
  7.9 0.0 all-gather.6.cloned.1.call-start
  8.0 1.2 slice.54
  9.2 0.8 reshape.93
  10.0 0.8 reduce-window.4
  10.8 0.6 compare_reduce_fusion
  12.1 0.6 fusion.5
  13.4 0.6 fusion.9
  15.9 0.1 select_reduce_fusion
  16.0 0.1 copy.41
  16.1 0.1 copy.42
  16.2 0.1 fusion.6
  16.3 0.1 copy.40
  16.4 0.1 slice.52
  16.4 0.2 slice_reduce_fusion
  16.6 0.1 add_bitcast_fusion
  16.7 0.1 copy.39
  16.8 2.0 %copy.43.fn_ref = bf16[2048,96]{1,0:T(8,128)(2,1)} copy(bf16[2048,96]{0,1:T(8,128)(2,1)} %param.32) | data formatting | bytes 786432 | tf_op args[10]
  18.8 0.0 copy-done.7
  18.8 1.1 copy.44.sn_ref
  19.9 0.7 stack.16.scal_ref
  20.6 0.0 copy-done.8
  20.6 0.1 slice_compare_fusion
  20.6 0.1 add_convert_fusion.1
  20.7 0.1 pad_add_fusion
  20.8 11.2 %all-gather.4.cloned.1.call-done.x_ref = bf16[384,2048]{1,0:T(8,128)(2,1)} async-done(((bf16[384,512]{1,0:T(8,128)(2,1)}), bf16[384,2048]{1,0:T(8,128)(2,1)}) %all-gather.4.cloned.1.call-update) | async-done | bytes 1572880 | tf_op jit(solution)/shard_map/all_gather | solution.py:350
  32.0 0.8 slice.63
  32.8 3.4 %collective-permute-start = (bf16[1,2048]{1,0:T(2,128)(2,1)S(1)}, bf16[1,2048]{1,0:T(2,128)(2,1)S(1)}, u32[]{:S(2)}, u32[]{:S(2)}) collective-permute-start(bf16[1,2048]{1,0:T(2,128)(2,1)S(1)} %slice.63), channel_id=1, source_target_pairs={{0,4},{4,8},{8,12},{12,16},{16,20},{20,24},{24,28},{1,5},{5,9},{9,... | collective-permute-start | bytes 12296 | tf_op jit(solution)/shard_map/ppermute | solution.py:316
  36.1 1.4 convert_reduce_fusion
  38.2 1.4 multiply_reduce_fusion
  40.3 0.7 fusion.3
  41.0 0.0 collective-permute-done.row_ref
  41.0 0.0 copy-start.9
  41.0 0.6 broadcast_in_dim.80.epr_ref
  41.6 0.8 broadcast_in_dim.72.cont_ref
  42.4 0.8 broadcast_in_dim.79.epc_ref
  43.2 0.0 copy-done.9
  43.2 33.7 %shard_map.229 = (f32[384,512]{1,0:T(8,128)}, f32[384,512]{1,0:T(8,128)}, f32[384,512]{1,0:T(8,128)}, f32[6,4,128,128]{3,2,1,0:T(8,128)}, f32[6,4,128,128]{3,2,1...) custom-call(s32[6,6]{1,0:T(8,128)} %stack.16.scal_ref, ...), custom_call_target="tpu_custom_call" | custom-call | tf_op jit(solution)/shard_map/pallas_call | solution.py:422
  76.9 1.6 fusion.1
  78.5 0.0 all-gather.6.cloned.1.call-update
  78.6 0.0 copy-start.1
  78.6 0.0 copy-start.5
  78.6 0.0 reduce-scatter.2.cloned.1.call-start
  78.6 0.0 copy-done.10
  78.7 0.1 pad_add_fusion.1.scal_ref
  78.7 44.0 %all-gather.6.cloned.1.call-done = bf16[6272,128]{1,0:T(8,128)(2,1)} async-done(((bf16[784,128]{1,0:T(8,128)(2,1)}), bf16[6272,128]{1,0:T(8,128)(2,1)}) %all-gather.6.cloned.1.call-update) | async-done | bytes 1605648 | tf_op jit(solution)/shard_map/all_gather | solution.py:469
  122.7 1.7 slice.64
  124.4 0.1 copy-done.3
  124.6 0.2 copy-done.4
  124.8 12.5 %shard_map.230 = (bf16[384,512]{1,0:T(8,128)(2,1)S(1)}, f32[4,64,128]{2,1,0:T(8,128)S(1)}) custom-call(s32[5]{0:T(128)S(1)} %pad_add_fusion.1.scal_ref, bf16[8,3,4,64,128]{4,3,2,1,0:T(8,128)(2,1)S(1)} %bitcast.44, f32[384,512]{1,0:T(8,128)S(1)} %copy-done.1, f32[384,512]{1,0:T(8,128)S(1)} %copy-done.2, f32[384,512]{1,0:T(8,128)S(1)} %copy-done.3, ...), custom_call_target="tpu_custom_call" | custom-call | tf_op jit(solution)/shard_map/pallas_call | solution.py:474
  137.3 2.1 %convolution_convert_fusion = bf16[384,2048]{1,0:T(8,128)(2,1)} fusion(bf16[384,512]{1,0:T(8,128)(2,1)S(1)} %get-tuple-element.19, bf16[512,2048]{1,0:T(8,128)(2,1)S(1)} %copy-done), kind=kOutput, calls=%fused_computation | convolution fusion | flops 806092800 | bytes 4063232 | tf_op jit(solution)/shard_map/dot_general | solution.py:504
  139.4 0.0 reduce-scatter.2.cloned.1.call-update
  139.5 0.6 fusion.7
  142.4 0.6 fusion.8
  145.4 0.7 slice_bitcast_fusion
  146.2 0.2 reshape.97
  146.4 0.7 copy.45
  147.1 0.6 broadcast_select_fusion.1
  147.7 18.9 %reduce-scatter.2.cloned.1.call-done = bf16[384,512]{1,0:T(8,128)(2,1)} async-done(((bf16[384,2048]{1,0:T(8,128)(2,1)}), bf16[384,512]{1,0:T(8,128)(2,1)}) %reduce-scatter.2.cloned.1.call-update) | async-done | bytes 393232 | tf_op jit(solution)/shard_map/reduce_scatter | solution.py:505
  166.6 1.8 %add_convert_fusion = bf16[384,512]{1,0:T(8,128)(2,1)} fusion(bf16[384,512]{1,0:T(8,128)(2,1)S(1)} %copy-done.6, bf16[384,512]{1,0:T(8,128)(2,1)} %reduce-scatter.2.cloned.1.call-done), kind=kLoop, calls=%fused_computation.1 | loop fusion | flops 786432 | bytes 1179648 | tf_op jit(solution)/shard_map/convert_element_type | solution.py:508
  (15 shorter events, 0.0 us)
Async XLA Ops:
  7.2 130.1 %copy-start = (bf16[512,2048]{1,0:T(8,128)(2,1)S(1)}, bf16[512,2048]{1,0:T(8,128)(2,1)}, u32[]{:S(2)}) copy-start(bf16[512,2048]{1,0:T(8,128)(2,1)} %param.31) | copy-start | bytes 6291460
  7.2 13.4 %copy-start.8 = (s32[384]{0:T(512)S(1)}, s32[384]{0:T(512)}, u32[]{:S(2)}) copy-start(s32[384]{0:T(512)} %param.23) | copy-start | bytes 4612
  7.2 11.6 %copy-start.7 = (bf16[2048,96]{0,1:T(8,128)(2,1)S(1)}, bf16[2048,96]{0,1:T(8,128)(2,1)}, u32[]{:S(2)}) copy-start(bf16[2048,96]{0,1:T(8,128)(2,1)} %param.35) | copy-start | bytes 1179652
  7.2 24.8 %all-gather.4.cloned.1.call-start = ((), (), s32[]{:S(2)}) async-start(), calls=%async_computation.1 | async-start | bytes 1966080 | tf_op jit(solution)/shard_map/all_gather | solution.py:350
  7.9 114.8 %all-gather.6.cloned.1.call-start = ((), (), s32[]{:S(2)}) async-start(), calls=%async_computation.3 | async-start | bytes 1806336 | tf_op jit(solution)/shard_map/all_gather | solution.py:469
  32.8 8.2 %collective-permute-start = (bf16[1,2048]{1,0:T(2,128)(2,1)S(1)}, bf16[1,2048]{1,0:T(2,128)(2,1)S(1)}, u32[]{:S(2)}, u32[]{:S(2)}) collective-permute-start(bf16[1,2048]{1,0:T(2,128)(2,1)S(1)} %slice.63), channel_id=1, source_target_pairs={{0,4},{4,8},{8,12},{12,16},{16,20},{20,24},{24,28},{1,5},{5,9},{9,... | collective-permute-start | bytes 12296 | tf_op jit(solution)/shard_map/ppermute | solution.py:316
  41.0 2.2 %copy-start.9 = (bf16[1,2048]{1,0:T(2,128)(2,1)}, bf16[1,2048]{1,0:T(2,128)(2,1)S(1)}, u32[]{:S(2)}) copy-start(bf16[1,2048]{1,0:T(2,128)(2,1)S(1)} %collective-permute-done.row_ref) | copy-start | bytes 12292
  43.2 35.5 %copy-start.10 = (s32[2]{0:T(128)S(1)}, s32[2]{0:T(128)}, u32[]{:S(2)}) copy-start(s32[2]{0:T(128)} %param.25) | copy-start | bytes 28
  78.6 45.8 %copy-start.1 = (f32[384,512]{1,0:T(8,128)S(1)}, f32[384,512]{1,0:T(8,128)}, u32[]{:S(2)}) copy-start(f32[384,512]{1,0:T(8,128)} %get-tuple-element.13.y_ref) | copy-start | bytes 2359300
  78.6 45.8 %copy-start.5 = (f32[512]{0:T(512)S(1)}, f32[512]{0:T(512)}, u32[]{:S(2)}) copy-start(f32[512]{0:T(512)} %param.43) | copy-start | bytes 6148
  78.6 88.0 %reduce-scatter.2.cloned.1.call-start = ((), (), s32[]{:S(2)}) async-start(), calls=%async_computation.2 | async-start | bytes 1966080 | tf_op jit(solution)/shard_map/reduce_scatter | solution.py:505
  122.7 1.7 copy-start.2
  122.7 1.8 %copy-start.3 = (f32[384,512]{1,0:T(8,128)S(1)}, f32[384,512]{1,0:T(8,128)}, u32[]{:S(2)}) copy-start(f32[384,512]{1,0:T(8,128)} %get-tuple-element.15.bonus_ref) | copy-start | bytes 2359300
  122.7 2.1 %copy-start.4 = (f32[384,512]{1,0:T(8,128)S(1)}, f32[384,512]{1,0:T(8,128)}, u32[]{:S(2)}) copy-start(f32[384,512]{1,0:T(8,128)} %get-tuple-element.16.gate_ref) | copy-start | bytes 2359300
  139.4 27.2 %copy-start.6 = (bf16[384,512]{1,0:T(8,128)(2,1)S(1)}, bf16[384,512]{1,0:T(8,128)(2,1)}, u32[]{:S(2)}) copy-start(bf16[384,512]{1,0:T(8,128)(2,1)} %param.22) | copy-start | bytes 1179652
Sparse Core Ops, SparseCore 0:
  9.6 22.3 all-gather.3
  78.7 43.9 all-gather.5
  139.6 26.9 reduce-scatter.1

commit v3 on v2

--- a/solution.py
+++ b/solution.py
@@ -245,58 +245,102 @@
             kept = jnp.where(e_end == i["e_in"], 1.0, 0.0).astype(F32)
             a_end, b_end = maps(uw, i, here, grow, kept)
             ended = dot3(earlier, a_end)
-            maps_ref[0, p] = fold(ended[:PAIR]).astype(BF16)
-            maps_ref[2, p] = fold(ended[PAIR:] + b_end).astype(BF16)
+            maps_ref[3, p] = fold(ended[:PAIR])
+            maps_ref[2, p] = fold(ended[PAIR:] + b_end)
 
     @pl.when(step == last_step)
     def _():
         for p in range(pairs):
-            maps_ref[1, p] = fold(run_ref[p, PAIR:]).astype(BF16)
-
-        @pl.when(scal_ref[0, 5] == 0)
-        def _():
-            for p in range(pairs):
-                maps_ref[0, p] = fold(run_ref[p, :PAIR]).astype(BF16)
+            maps_ref[0, p] = fold(run_ref[p, :PAIR])
+            maps_ref[1, p] = fold(run_ref[p, PAIR:])
+
+
+def chain_kernel(maps_ref, state_ref, end_ref, going, coming, send_sem, recv_sem):
+    me = lax.axis_index("seq")
+    n = lax.axis_size("seq")
+    pairs = maps_ref.shape[1]
+    right = lax.rem(me + 1, n)
+    left = lax.rem(me + n - 1, n)
+    barrier = pltpu.get_barrier_semaphore()
+
+    @pl.when(me > 0)
+    def _():
+        pl.semaphore_signal(
+            barrier, inc=1, device_id={"seq": left}, device_id_type=pl.DeviceIdType.MESH
+        )
+
+    @pl.when(me < n - 1)
+    def _():
+        pl.semaphore_signal(
+            barrier, inc=1, device_id={"seq": right}, device_id_type=pl.DeviceIdType.MESH
+        )
+
+    @pl.when(me == 0)
+    def _():
+        coming[...] = jnp.zeros_like(coming)
+
+    def factor(which, p):
+        return jnp.concatenate(split(two(maps_ref[which, p])), axis=0)
+
+    factors = [factor(0, p) for p in range(pairs)]
+
+    @pl.when((me > 0) & (me < n - 1))
+    def _():
+        pl.semaphore_wait(barrier, 2)
+
+    @pl.when((me == 0) | (me == n - 1))
+    def _():
+        pl.semaphore_wait(barrier, 1)
+
+    def advance(p, right_side, which):
+        state = two(coming[p].astype(F32)).astype(BF16)
+        moved = lax.dot_general(
+            jnp.concatenate([state, state], axis=1), right_side, NN, preferred_element_type=F32
+        )
+        return (fold(moved) + maps_ref[which, p]).astype(BF16)
+
+    copies = [
+        pltpu.make_async_remote_copy(
+            src_ref=going.at[p],
+            dst_ref=coming.at[p],
+            send_sem=send_sem.at[p],
+            recv_sem=recv_sem.at[p],
+            device_id={"seq": right},
+            device_id_type=pl.DeviceIdType.MESH,
+        )
+        for p in range(pairs)
+    ]
+    for p in range(pairs):
+
+        @pl.when(me > 0)
+        def _(p=p):
+            copies[p].wait_recv()
+
+        going[p] = advance(p, factors[p], 1)
+
+        @pl.when(me < n - 1)
+        def _(p=p):
+            copies[p].start()
+
+    for p in range(pairs):
+        state_ref[p] = coming[p].astype(F32)
+        end_ref[p] = advance(p, factor(3, p), 2)
+
+    @pl.when(me < n - 1)
+    def _():
+        for p in range(pairs):
+            copies[p].wait_send()
 
 
 def read_kernel(
-    scal_ref, all_ref, y_ref, z_ref, bonus_ref, gate_ref, gain_ref, a_ref, b_ref,
-    vis_ref, final_ref, state_ref, mine_ref,
+    state_ref, y_ref, z_ref, bonus_ref, gate_ref, gain_ref, a_ref, b_ref, vis_ref, mine_ref
 ):
-    c = pl.program_id(0)
     pairs = y_ref.shape[1] // PAIR
-    count = all_ref.shape[0]
-    position = scal_ref[0]
-
-    @pl.when(c == 0)
-    def _():
-        final_ref[...] = jnp.zeros_like(final_ref)
-        state_ref[...] = jnp.zeros_like(state_ref)
-
-        def hop(d, carry):
-            @pl.when(d == position)
-            def _():
-                mine_ref[...] = state_ref[...]
-
-            holds = (d == scal_ref[1]) | (d == scal_ref[2])
-            owner = jnp.where(d == scal_ref[1], scal_ref[3], scal_ref[4])
-
-            for p in range(pairs):
-                state = state_ref[p]
-                high, low = split(state)
-                a_map = two(all_ref[d, 0, p].astype(F32)).astype(BF16)
-                moved = lax.dot_general(high, a_map, NN, preferred_element_type=F32)
-                moved = moved + lax.dot_general(low, a_map, NN, preferred_element_type=F32)
-
-                @pl.when(holds & (owner == position))
-                def _():
-                    final_ref[p] = fold(moved) + all_ref[d, 2, p].astype(F32)
-
-                local = two(all_ref[d, 1, p].astype(F32))
-                state_ref[p] = jnp.where(holds, 0.0, moved) + local
-            return carry
-
-        lax.fori_loop(0, count, hop, 0)
+
+    @pl.when(pl.program_id(0) == 0)
+    def _():
+        for p in range(pairs):
+            mine_ref[p] = two(state_ref[p])
 
     ones = head_ones()
     for p in range(pairs):
@@ -346,7 +390,6 @@
     chunks = tokens // CHUNK
     position = lax.axis_index("seq")
     column = lax.axis_index("tp")
-    n_seq = lax.axis_size("seq")
     gathered = lax.all_gather(layer_activation, "tp", axis=1, tiled=True)
     arrived = from_behind(gathered[-1:], "seq", 1)
     bounds = jnp.cumsum(sequence_extents)
@@ -434,7 +477,7 @@
             wide(),
             mats(SUBS),
             mats(SUBS),
-            pl.BlockSpec((3, pairs, HEAD, PAIR), lambda c: (0, 0, 0, 0)),
+            pl.BlockSpec((4, pairs, HEAD, PAIR), lambda c: (0, 0, 0, 0)),
             pl.BlockSpec((tokens, width), lambda c: (0, 0)),
         ],
         out_shape=[
@@ -443,7 +486,7 @@
             big,
             mat,
             mat,
-            jax.ShapeDtypeStruct((3, pairs, HEAD, PAIR), BF16),
+            jax.ShapeDtypeStruct((4, pairs, HEAD, PAIR), F32),
             big,
         ],
         scratch_shapes=[
@@ -459,24 +502,37 @@
     row_raw = lax.dynamic_slice(gathered, (local_end, 0), (1, features)).astype(F32)
     row_norm = rms_rows(row_raw, entry_layernorm_coef).astype(BF16)
     row_end = lax.dynamic_slice(row_norm, (0, column * width), (1, width))
+    vmem = pl.BlockSpec(memory_space=pltpu.VMEM)
+    state_in, end_state = pl.pallas_call(
+        chain_kernel,
+        in_specs=[vmem],
+        out_specs=[vmem, vmem],
+        out_shape=[
+            jax.ShapeDtypeStruct((pairs, HEAD, PAIR), F32),
+            jax.ShapeDtypeStruct((pairs, HEAD, PAIR), BF16),
+        ],
+        scratch_shapes=[
+            pltpu.VMEM((pairs, HEAD, PAIR), BF16),
+            pltpu.VMEM((pairs, HEAD, PAIR), BF16),
+            pltpu.SemaphoreType.DMA((pairs,)),
+            pltpu.SemaphoreType.DMA((pairs,)),
+        ],
+        compiler_params=pltpu.CompilerParams(collective_id=0, has_side_effects=True),
+    )(maps)
+    high = pairs * HEAD
     sent = jnp.concatenate(
         [
-            maps.reshape(3 * pairs * HEAD, PAIR),
+            end_state.reshape(high, PAIR),
             jnp.pad(row_end.reshape(pairs, PAIR), ((0, 16 - pairs), (0, 0))),
         ],
         axis=0,
     )
     everyone = lax.all_gather(sent, "seq", axis=0, tiled=False)
-    all_maps = everyone[:, : 3 * pairs * HEAD].reshape(n_seq, 3, pairs, HEAD, PAIR)
-    rows = everyone[:, 3 * pairs * HEAD : 3 * pairs * HEAD + pairs].reshape(n_seq, width)
-
-    facts = jnp.concatenate([position[None], holders, destination_slots]).astype(jnp.int32)
-    visible, final_fold = pl.pallas_call(
+    visible = pl.pallas_call(
         read_kernel,
         grid=(chunks,),
         in_specs=[
-            smem,
-            pl.BlockSpec((n_seq, 3, pairs, HEAD, PAIR), lambda c: (0, 0, 0, 0, 0), pipeline_mode=pl.Buffered(1)),
+            pl.BlockSpec((pairs, HEAD, PAIR), lambda c: (0, 0, 0)),
             tall(),
             tall(),
             tall(),
@@ -485,21 +541,24 @@
             mats(1),
             mats(1),
         ],
-        out_specs=[tall(), pl.BlockSpec((pairs, HEAD, PAIR), lambda c: (0, 0, 0))],
-        out_shape=[
-            jax.ShapeDtypeStruct((tokens, width), BF16),
-            jax.ShapeDtypeStruct((pairs, HEAD, PAIR), F32),
-        ],
-        scratch_shapes=[pltpu.VMEM((pairs, PAIR, PAIR), F32), pltpu.VMEM((pairs, PAIR, PAIR), F32)],
+        out_specs=tall(),
+        out_shape=jax.ShapeDtypeStruct((tokens, width), BF16),
+        scratch_shapes=[pltpu.VMEM((pairs, PAIR, PAIR), F32)],
         compiler_params=pltpu.CompilerParams(vmem_limit_bytes=48 << 20),
-    )(facts, all_maps, y, z, bonus, gating_signal, group_layernorm_coef[None], a_maps, b_maps)
-
-    final_states = final_fold.reshape(pairs, HEAD, 2, HEAD).transpose(0, 2, 1, 3)
-    final_states = final_states.reshape(1, 2 * pairs, HEAD, HEAD)
+        cost_estimate=pl.CostEstimate(
+            flops=2 * tokens * width * 1024, bytes_accessed=24 * tokens * width, transcendentals=0
+        ),
+    )(state_in, y, z, bonus, gating_signal, group_layernorm_coef[None], a_maps, b_maps)
+
+    final_fold = jnp.zeros((high, PAIR), BF16)
     final_rows = jnp.zeros((1, width), BF16)
     for prompt in range(PROMPTS):
-        got = lax.dynamic_slice(rows, (holders[prompt], 0), (1, width))
-        final_rows = jnp.where(position == destination_slots[prompt], got, final_rows)
+        got = lax.dynamic_index_in_dim(everyone, holders[prompt], 0, keepdims=False)
+        owner = position == destination_slots[prompt]
+        final_fold = jnp.where(owner, got[:high], final_fold)
+        final_rows = jnp.where(owner, got[high : high + pairs].reshape(1, width), final_rows)
+    final_states = final_fold.astype(F32).reshape(pairs, HEAD, 2, HEAD).transpose(0, 2, 1, 3)
+    final_states = final_states.reshape(1, 2 * pairs, HEAD, HEAD)
 
     partial_value = jnp.dot(visible, readout_matrix, preferred_element_type=F32)
     summed = lax.psum_scatter(

time: 176 us -> 172 us (0.977)
  waiting for transfers between devices: 74.8 us -> 16.7 us
  blocking collectives: 0 us -> 49.4 us
  local copies, waits for them, and re-layouts: 14.8 us -> 20.4 us
    all_gather x0 -> x1, blocking collectives: none -> 49.4 us  [on_device(): everyone = lax.all_gather(sent, 'seq', axis=0, tiled=False)]
    all_gather x1 -> x0, waiting for transfers between devices: 44 us -> none  [on_device(): everyone = lax.all_gather(sent, 'seq', axis=0, tiled=False)]
    reduce_scatter x1, waiting for transfers between devices: 18.9 us -> 0.01 us  [on_device(): lax.psum_scatter(partial_value.astype(BF16), 'tp', scatter_dimension=1, t...]
    unnamed x26 -> x29, local copies, waits for them, and re-layouts: 4.24 us -> 11.6 us
    all_gather x1, waiting for transfers between devices: 11.2 us -> 16 us  [on_device(): gathered = lax.all_gather(layer_activation, 'tp', axis=1, tiled=True)]
    pallas_call x1 -> x2, Pallas kernels: 12.5 us -> 12.3 us  [the longest x1 6.9 us: on_device(): pl.pallas_call(read_kernel, grid=(chunks,), in_specs=[pl.BlockSpec((pairs...]
  transfers between devices with their start and end apart: 4 -> 3, of which waited for: 3 -> 1; matrix products, arithmetic and copies ran while one was open for 9% -> 10% of each run, Pallas kernels for 0% -> 0%
where the time goes in v3:
time: 172 us; the launch traced here: 171 us
  blocking collectives  49.4 us (29%)
  Pallas kernels  46.3 us (27%)
  between operations  23.9 us (14%)
  local copies, waits for them, and re-layouts  20.4 us (12%)
  waiting for transfers between devices  16.7 us (10%)
  other arithmetic  8.76 us (5%)
  starting transfers between devices  3.45 us (2%)
  matrix products  2.13 us (1%)
    all_gather x1, blocking collectives, on_device(): everyone = lax.all_gather(sent, 'seq', axis=0, tiled=False)  49.4 us
    pallas_call x1, Pallas kernels, on_device(): pl.pallas_call(chunk_kernel, grid=(chunks // SUBS,), in_specs=[smem] + [w...  34 us
    all_gather x1, waiting for transfers between devices, on_device(): gathered = lax.all_gather(layer_activation, 'tp', axis=1, tiled=True)  16 us
    unnamed x29, local copies, waits for them, and re-layouts  11.6 us
    pallas_call x1, Pallas kernels, on_device(): pl.pallas_call(read_kernel, grid=(chunks,), in_specs=[pl.BlockSpec((pairs...  6.9 us
    pallas_call x1, Pallas kernels, on_device(): pl.pallas_call(chain_kernel, in_specs=[vmem], out_specs=[vmem, vmem], out...  5.4 us
  transfers between devices with their start and end apart: 3, of which 1 were waited for; matrix products, arithmetic and copies ran while one was open for 10% of the time, Pallas kernels for 0%

profile of v3, /device:TPU:0, one launch (start us, length us, event | category | flops | bytes accessed | tf_op | source)
XLA Modules:
  0.0 171.1 jit_solution(13842505907598166932)
XLA Ops:
  7.2 0.0 copy-start
  7.2 0.0 copy-start.10
  7.2 0.0 all-gather.3.cloned.1.call-start
  7.2 0.7 all-gather.3.cloned.1.call-update
  7.9 0.0 reduce-scatter.2.cloned.1.call-start
  8.0 0.8 reshape.134
  8.7 1.2 slice.64
  9.9 0.8 reduce-window.4
  10.8 0.6 fusion.14
  13.3 0.8 slice_compare_fusion
  14.1 0.1 add_convert_fusion.1
  14.2 0.7 fusion.10
  14.9 0.6 compare_reduce_fusion
  15.5 0.1 pad_add_fusion
  15.6 0.2 slice_reduce_fusion
  15.8 0.1 select_reduce_fusion
  15.9 0.1 fusion.11
  16.0 16.0 %all-gather.3.cloned.1.call-done.x_ref = bf16[384,2048]{1,0:T(8,128)(2,1)} async-done(((bf16[384,512]{1,0:T(8,128)(2,1)}), bf16[384,2048]{1,0:T(8,128)(2,1)}) %all-gather.3.cloned.1.call-update) | async-done | bytes 1572880 | tf_op jit(solution)/shard_map/all_gather | solution.py:393
  32.0 0.8 slice.75
  32.7 3.4 %collective-permute-start = (bf16[1,2048]{1,0:T(2,128)(2,1)S(1)}, bf16[1,2048]{1,0:T(2,128)(2,1)S(1)}, u32[]{:S(2)}, u32[]{:S(2)}) collective-permute-start(bf16[1,2048]{1,0:T(2,128)(2,1)S(1)} %slice.75), channel_id=1, source_target_pairs={{0,4},{4,8},{8,12},{12,16},{16,20},{20,24},{24,28},{1,5},{5,9},{9,... | collective-permute-start | bytes 12296 | tf_op jit(solution)/shard_map/ppermute | solution.py:360
  36.1 0.1 add_bitcast_fusion
  36.2 0.1 slice.62
  36.3 0.1 copy.39
  37.0 0.1 copy.41
  37.1 0.1 copy.42
  37.2 0.1 copy.40
  37.3 2.1 %copy.43.fn_ref = bf16[2048,96]{1,0:T(8,128)(2,1)} copy(bf16[2048,96]{0,1:T(8,128)(2,1)} %param.32) | data formatting | bytes 786432 | tf_op args[10]
  39.4 2.1 %copy.44.sn_ref = bf16[2048,96]{1,0:T(8,128)(2,1)} copy(bf16[2048,96]{0,1:T(8,128)(2,1)} %param.35) | data formatting | bytes 786432 | tf_op args[13]
  41.4 0.7 stack.16.scal_ref
  42.1 0.0 collective-permute-done.row_ref
  42.1 0.8 broadcast_in_dim.71.cont_ref
  42.9 0.6 broadcast_in_dim.79.epr_ref
  43.5 0.0 copy-done.10
  43.5 0.8 broadcast_in_dim.78.epc_ref
  44.3 0.0 copy-done.11
  44.3 34.0 %shard_map.229 = (f32[384,512]{1,0:T(8,128)}, f32[384,512]{1,0:T(8,128)}, f32[384,512]{1,0:T(8,128)}, f32[6,4,128,128]{3,2,1,0:T(8,128)}, f32[6,4,128,128]{3,2,1...) custom-call(s32[6,6]{1,0:T(8,128)} %stack.16.scal_ref, bf16[384,2048]{1,0:T(8,128)(2,1)} %all-gather.3.cloned.1.call-done.x_ref, ...), custom_call_target="tpu_custom_call" | custom-call | tf_op jit(solution)/shard_map/pallas_call | solution.py:465
  78.3 5.4 %shard_map.230 = (f32[4,64,128]{2,1,0:T(8,128)}, bf16[4,64,128]{2,1,0:T(8,128)(2,1)}) custom-call(f32[4,4,64,128]{3,2,1,0:T(8,128)} %get-tuple-element.12.maps_ref), custom_call_target="tpu_custom_call" | custom-call | tf_op jit(solution)/shard_map/pallas_call | solution.py:506
  83.7 0.0 copy-done.7
  83.7 0.0 copy-start.1
  83.7 1.4 copy-done.1
  85.1 1.1 copy-done.2
  86.3 1.1 copy-done.3
  87.4 1.1 copy-done.4
  88.5 1.1 copy-done.5
  89.7 0.9 copy-done.6
  90.6 6.9 %shard_map.231 = bf16[384,512]{1,0:T(8,128)(2,1)S(1)} custom-call(f32[4,64,128]{2,1,0:T(8,128)S(1)} %copy-done.6, f32[384,512]{1,0:T(8,128)S(1)} %copy-done.2, f32[384,512]{1,0:T(8,128)S(1)} %copy-done.3, f32[384,512]{1,0:T(8,128)S(1)} %copy-done.4, f32[384,512]{1,0:T(8,128)S(1)} %copy-done.5, f32[1,512]{1,0:T(1,128)S(1)} %bitcast.43, ...), custom_call_target="tpu_custom_call" | custom-call | flops 402653184 | bytes 4718592 | tf_op jit(solution)/shard_map/pallas_call | solution.py:531
  97.5 0.0 copy-done
  97.5 0.0 copy-start.12
  97.5 0.0 copy-start.9
  97.5 2.1 %convolution_convert_fusion = bf16[384,2048]{1,0:T(8,128)(2,1)} fusion(bf16[384,512]{1,0:T(8,128)(2,1)S(1)} %shard_map.231, bf16[512,2048]{1,0:T(8,128)(2,1)S(1)} %copy-done), kind=kOutput, calls=%fused_computation | convolution fusion | flops 806092800 | bytes 4063232 | tf_op jit(solution)/shard_map/dot_general | solution.py:563
  99.6 0.0 reduce-scatter.2.cloned.1.call-update
  99.7 0.6 fusion.13
  103.5 0.0 copy-done.12
  103.5 0.6 fusion.12
  106.6 1.4 convert_reduce_fusion
  108.6 1.4 multiply_reduce_fusion
  110.7 0.7 fusion.5
  111.4 0.0 copy-done.9
  111.4 49.4 %all-gather = bf16[2176,128]{1,0:T(8,128)(2,1)S(1)} all-gather(bf16[272,128]{1,0:T(8,128)(2,1)S(1)} %fusion.1), channel_id=2, replica_groups=mesh['seq'=8,'tp'=4] {'seq'}, dimensions={0}, use_global_device_ids=true | all-gather | bytes 626688 | tf_op jit(solution)/shard_map/all_gather | solution.py:530
  160.9 0.2 reshape.144
  161.1 0.7 copy.45
  161.8 0.6 copy.48
  162.4 0.0 copy-done.8
  162.4 1.8 %add_convert_fusion = bf16[384,512]{1,0:T(8,128)(2,1)} fusion(bf16[384,512]{1,0:T(8,128)(2,1)S(1)} %copy-done.8, bf16[384,512]{1,0:T(8,128)(2,1)} %reduce-scatter.2.cloned.1.call-done), kind=kLoop, calls=%fused_computation.1 | loop fusion | flops 786432 | bytes 1179648 | tf_op jit(solution)/shard_map/convert_element_type | solution.py:567
  (16 shorter events, 0.1 us)
Async XLA Ops:
  7.2 90.3 %copy-start = (bf16[512,2048]{1,0:T(8,128)(2,1)S(1)}, bf16[512,2048]{1,0:T(8,128)(2,1)}, u32[]{:S(2)}) copy-start(bf16[512,2048]{1,0:T(8,128)(2,1)} %param.31) | copy-start | bytes 6291460
  7.2 36.3 %copy-start.10 = (s32[384]{0:T(512)S(1)}, s32[384]{0:T(512)}, u32[]{:S(2)}) copy-start(s32[384]{0:T(512)} %param.23) | copy-start | bytes 4612
  7.2 24.8 %all-gather.3.cloned.1.call-start = ((), (), s32[]{:S(2)}) async-start(), calls=%async_computation.1 | async-start | bytes 1966080 | tf_op jit(solution)/shard_map/all_gather | solution.py:393
  7.9 154.5 %reduce-scatter.2.cloned.1.call-start = ((), (), s32[]{:S(2)}) async-start(), calls=%async_computation.2 | async-start | bytes 1966080 | tf_op jit(solution)/shard_map/reduce_scatter | solution.py:564
  32.7 9.3 %collective-permute-start = (bf16[1,2048]{1,0:T(2,128)(2,1)S(1)}, bf16[1,2048]{1,0:T(2,128)(2,1)S(1)}, u32[]{:S(2)}, u32[]{:S(2)}) collective-permute-start(bf16[1,2048]{1,0:T(2,128)(2,1)S(1)} %slice.75), channel_id=1, source_target_pairs={{0,4},{4,8},{8,12},{12,16},{16,20},{20,24},{24,28},{1,5},{5,9},{9,... | collective-permute-start | bytes 12296 | tf_op jit(solution)/shard_map/ppermute | solution.py:360
  42.1 2.2 %copy-start.11 = (bf16[1,2048]{1,0:T(2,128)(2,1)}, bf16[1,2048]{1,0:T(2,128)(2,1)S(1)}, u32[]{:S(2)}) copy-start(bf16[1,2048]{1,0:T(2,128)(2,1)S(1)} %collective-permute-done.row_ref) | copy-start | bytes 12292
  44.3 39.4 %copy-start.7 = (f32[512]{0:T(512)S(1)}, f32[512]{0:T(512)}, u32[]{:S(2)}) copy-start(f32[512]{0:T(512)} %param.43) | copy-start | bytes 6148
  83.7 1.4 copy-start.1
  85.1 1.1 copy-start.2
  86.3 1.1 copy-start.3
  87.4 1.1 copy-start.4
  88.5 1.1 copy-start.5
  89.7 0.9 copy-start.6
  97.5 6.0 %copy-start.12 = (s32[2]{0:T(128)S(1)}, s32[2]{0:T(128)}, u32[]{:S(2)}) copy-start(s32[2]{0:T(128)} %param.25) | copy-start | bytes 28
  97.5 13.9 %copy-start.9 = (bf16[4,64,128]{2,1,0:T(8,128)(2,1)S(1)}, bf16[4,64,128]{2,1,0:T(8,128)(2,1)}, u32[]{:S(2)}) copy-start(bf16[4,64,128]{2,1,0:T(8,128)(2,1)} %get-tuple-element.20) | copy-start | bytes 196612
  99.6 62.7 %copy-start.8 = (bf16[384,512]{1,0:T(8,128)(2,1)S(1)}, bf16[384,512]{1,0:T(8,128)(2,1)}, u32[]{:S(2)}) copy-start(bf16[384,512]{1,0:T(8,128)(2,1)} %param.22) | copy-start | bytes 1179652
Sparse Core Ops, SparseCore 0:
  9.6 22.3 all-gather.2
  99.8 46.7 reduce-scatter.1
